TPU v7x, 1024 devices: a whole 4x8x16 slice. The times are simulated.
1024 devices in a mesh: sec: 4 (over z_hi), row: 8 (over y), col: 32 (over z_lo, x, core).
Axes of the slice: x: 4, y: 8, z: 16 (z_hi: 4, z_lo: 4; z = z_hi * 4 + z_lo), core: 2. Of those that a mesh axis runs over, the one named last changes fastest.
Arguments:
- labels: int32 [64, 512, 512], P('col', 'row', 'sec'), may hold values 0 or 1
- jitter: float32 [2, 64, 512, 512], P(None, 'col', 'row', 'sec'), may hold values from 0.5 to 1.5
- shells: int32 [512, 512], P('row', 'sec'), may hold values from 0 to 255, as said below
Outputs:
- populations: float32 [38, 64, 512, 512], P(None, 'col', 'row', 'sec')
- spectrum: float32 [64, 256], P('col')
Inputs may be any that keep to these rules, and one draw needn't show every extreme that they name: shells are radial bins of |k|: with kx' = kx for kx < 256, else kx - 512 (ky' likewise with 512), shells[kx, ky] = min(floor(sqrt(kx'^2 + ky'^2 + j)), 255), where j is 0 or 1 per wavevector (0 at k = 0); every label from 0 to 255 belongs to at least one wavevector.
All inputs are finite; a program needn't handle non-finite values. No bound on the sum of `labels` on one device may be relied on, other than what follows from the above.
Results may differ from a plain program's by a relative error of at most 0.002.
Values may be sent and summed in bfloat16 or wider, within the bound.
A program may use at most 32 MiB of HBM per device.

v0:
```python
import math

import jax
import jax.numpy as jnp
from jax import lax
from jax.sharding import PartitionSpec as P

NSHELL = 256


LATTICE = (
    (0, 0, 0),
    (1, 0, 0),
    (-1, 0, 0),
    (0, 1, 0),
    (0, -1, 0),
    (0, 0, 1),
    (0, 0, -1),
    (1, 1, 0),
    (-1, -1, 0),
    (1, -1, 0),
    (-1, 1, 0),
    (1, 0, 1),
    (-1, 0, -1),
    (1, 0, -1),
    (-1, 0, 1),
    (0, 1, 1),
    (0, -1, -1),
    (0, 1, -1),
    (0, -1, 1),
)
WEIGHTS = (1.0 / 3.0,) + (1.0 / 18.0,) * 6 + (1.0 / 36.0,) * 12


def with_halo(block, sides, width):
    for axis, dim in sides:
        count = lax.axis_size(axis)
        forward = [(i, i + 1) for i in range(count - 1)]
        forward.append((count - 1, 0))
        backward = [(target, source) for source, target in forward]
        low = lax.ppermute(
            lax.slice_in_dim(block, block.shape[dim] - width, None, axis=dim), axis, forward
        )
        high = lax.ppermute(lax.slice_in_dim(block, 0, width, axis=dim), axis, backward)
        block = jnp.concatenate([low, block, high], axis=dim)
    return block


def density_pair(labels, jitter):
    heavy_a = jnp.where(labels == 1, jnp.float32(1.0), jnp.float32(0.2))
    heavy_b = jnp.where(labels == 1, jnp.float32(0.2), jnp.float32(1.0))
    return jnp.stack([heavy_a * jitter[0], heavy_b * jitter[1]])


def pull_sums(padded):
    inner_z = padded.shape[1] - 2
    inner_x = padded.shape[2] - 2
    inner_y = padded.shape[3] - 2
    zeros_field = jnp.zeros((2, inner_z, inner_x, inner_y), jnp.float32)
    totals_axis = [zeros_field, zeros_field, zeros_field]
    for offsets, weight in zip(LATTICE[1:], WEIGHTS[1:]):
        shifted = padded[
            :,
            1 + offsets[2] : 1 + offsets[2] + inner_z,
            1 + offsets[0] : 1 + offsets[0] + inner_x,
            1 + offsets[1] : 1 + offsets[1] + inner_y,
        ]
        for axis_id in range(3):
            if offsets[axis_id] != 0:
                totals_axis[axis_id] = totals_axis[axis_id] + weight * offsets[axis_id] * shifted
    return jnp.stack(totals_axis, axis=1)


def relax_stack(densities, pull_terms):
    velocities = (-1.6 * pull_terms[1], -1.6 * pull_terms[0])
    term_list = []
    for component in range(2):
        velocity = velocities[component]
        density = densities[component]
        squared = velocity[0] * velocity[0] + velocity[1] * velocity[1] + velocity[2] * velocity[2]
        for offsets, weight in zip(LATTICE, WEIGHTS):
            projected = (
                offsets[0] * velocity[0] + offsets[1] * velocity[1] + offsets[2] * velocity[2]
            )
            term_list.append(
                weight
                * density
                * (1.0 + 1.25 * (3.0 * projected + 4.5 * projected * projected - 1.5 * squared))
            )
    return jnp.stack(term_list)


def movers(axis_id, sign):
    return [number for number in range(38) if LATTICE[number % 19][axis_id] == sign]


def edge_pack(stacked, dim, axis_id):
    length = stacked.shape[dim]
    leaving_low = jnp.stack(
        [lax.slice_in_dim(stacked[number], 0, 1, axis=dim - 1) for number in movers(axis_id, -1)]
    )
    leaving_high = jnp.stack(
        [
            lax.slice_in_dim(stacked[number], length - 1, length, axis=dim - 1)
            for number in movers(axis_id, 1)
        ]
    )
    return jnp.concatenate([leaving_low, leaving_high], axis=dim)


def edge_apply(stacked, rim, dim, axis_id):
    length = stacked.shape[dim]
    from_low = lax.slice_in_dim(rim, 0, 1, axis=dim)
    from_high = lax.slice_in_dim(rim, 3, 4, axis=dim)
    moved_list = [stacked[number] for number in range(38)]
    for place, number in enumerate(movers(axis_id, 1)):
        moved_list[number] = jnp.concatenate(
            [from_low[place], lax.slice_in_dim(stacked[number], 0, length - 1, axis=dim - 1)],
            axis=dim - 1,
        )
    for place, number in enumerate(movers(axis_id, -1)):
        moved_list[number] = jnp.concatenate(
            [lax.slice_in_dim(stacked[number], 1, length, axis=dim - 1), from_high[place]],
            axis=dim - 1,
        )
    return jnp.stack(moved_list)


def x_part(portion, first_kx, width_x, full_x):
    count_x = portion.shape[1]
    freq_x = first_kx + jnp.arange(width_x, dtype=jnp.int32)[:, None]
    pos_x = jnp.arange(count_x, dtype=jnp.int32)[None, :]
    angles = (freq_x * pos_x % full_x).astype(jnp.float32) * (2.0 * math.pi / full_x)
    table = jnp.concatenate(
        [jnp.cos(angles).astype(jnp.bfloat16), (-jnp.sin(angles)).astype(jnp.bfloat16)], 0
    )
    return jnp.einsum("kx,zxy->zky", table, portion, preferred_element_type=jnp.float32)


def y_part(portion, first_ky, width_x, width_y, full_y):
    count_y = portion.shape[2]
    pos_y = jnp.arange(count_y, dtype=jnp.int32)[:, None]
    freq_y = first_ky + jnp.arange(width_y, dtype=jnp.int32)[None, :]
    angles = (pos_y * freq_y % full_y).astype(jnp.float32) * (2.0 * math.pi / full_y)
    cos_y = jnp.cos(angles).astype(jnp.bfloat16)
    sin_y = jnp.sin(angles).astype(jnp.bfloat16)
    right_side = jnp.concatenate(
        [jnp.concatenate([cos_y, -sin_y], 1), jnp.concatenate([sin_y, cos_y], 1)], 0
    )
    left_side = jnp.concatenate([portion[:, :width_x], portion[:, width_x:]], axis=2)
    return jnp.einsum("zkv,vw->zkw", left_side, right_side, preferred_element_type=jnp.float32)


def on_device(labels, jitter, shells):
    depth_z, width_x, width_y = labels.shape
    densities = density_pair(labels, jitter)
    padded = with_halo(
        densities.astype(jnp.bfloat16), (("sec", 3), ("row", 2), ("col", 1)), 1
    ).astype(densities.dtype)
    pull_terms = pull_sums(padded)
    relaxed = relax_stack(densities, pull_terms)
    rim_x = with_halo(edge_pack(relaxed, 2, 0), (("row", 2),), 1)
    stepped = edge_apply(relaxed, rim_x, 2, 0)
    rim_y = with_halo(edge_pack(stepped, 3, 1), (("sec", 3),), 1)
    stepped = edge_apply(stepped, rim_y, 3, 1)
    rim_z = with_halo(edge_pack(stepped, 1, 2).astype(jnp.bfloat16), (("col", 1),), 1).astype(
        jnp.float32
    )
    populations = edge_apply(stepped, rim_z, 1, 2)
    order_b = (densities[0] - densities[1]).astype(jnp.bfloat16)
    full_x = width_x * lax.axis_size("row")
    full_y = width_y * lax.axis_size("sec")
    first_kx = lax.axis_index("row") * width_x
    first_ky = lax.axis_index("sec") * width_y
    rows_all = lax.all_gather(order_b, "row", axis=1, tiled=True)
    whole_plane = lax.all_gather(rows_all, "sec", axis=2, tiled=True)
    half_step = x_part(whole_plane, first_kx, width_x, full_x).astype(jnp.bfloat16)
    transform = y_part(half_step, first_ky, width_x, width_y, full_y)
    real_part = transform[..., :width_y]
    imag_part = transform[..., width_y:]
    power_map = real_part * real_part + imag_part * imag_part
    cell_count = width_x * width_y
    flat_shells = shells.reshape(cell_count)
    totals = jax.ops.segment_sum(
        power_map.reshape(depth_z, cell_count).T, flat_shells, num_segments=NSHELL
    )
    counts = jax.ops.segment_sum(
        jnp.ones((cell_count,), jnp.float32), flat_shells, num_segments=NSHELL
    )
    totals, counts = lax.psum((totals, counts), ("sec", "row"))
    spectrum = (totals / (counts[:, None] * float(full_x * full_y))).T
    return (populations, spectrum)


def solution(mesh):
    in_specs = (P("col", "row", "sec"), P(None, "col", "row", "sec"), P("row", "sec"))
    out_specs = (P(None, "col", "row", "sec"), P("col", None))
    return jax.shard_map(
        on_device, mesh=mesh, in_specs=in_specs, out_specs=out_specs, check_vma=False
    )
```

profile of v0, /device:TPU:64, one launch (start us, length us, event | category | flops | bytes accessed | tf_op | source)
XLA Modules:
  0.0 468.5 jit_solution(2949330641606856100)
XLA Ops:
  9.3 10.9 %collective-permute-start = (bf16[2,2,64,1]{3,1,2,0:T(2,128)(2,1)S(1)}, bf16[2,2,64,1]{3,1,2,0:T(2,128)(2,1)S(1)}, u32[]{:S(2)}, u32[]{:S(2)}) collective-permute-start(bf16[2,2,64,1]{3,1,2,0:T(2,128)(2,1)S(1)} %get-tuple-element.111), channel_id=1, source_target_pairs={{0,256},{256,512},{512,768},{768,0},{1,257},{257,513},{513,769},{7... | collective-permute-start | bytes 1544 | tf_op jit(solution)/shard_map/ppermute | solution.py:41
  20.2 8.3 %collective-permute-start.1 = (bf16[2,2,64,1]{3,1,2,0:T(2,128)(2,1)S(1)}, bf16[2,2,64,1]{3,1,2,0:T(2,128)(2,1)S(1)}, u32[]{:S(2)}, u32[]{:S(2)}) collective-permute-start(bf16[2,2,64,1]{3,1,2,0:T(2,128)(2,1)S(1)} %get-tuple-element.112), channel_id=1, source_target_pairs={{256,0},{512,256},{768,512},{0,768},{257,1},{513,257},{769,513},{1... | collective-permute-start | bytes 1544 | tf_op jit(solution)/shard_map/ppermute | solution.py:44
  28.5 28.5 %all_gather.6 = bf16[2,512,128]{2,1,0:T(8,128)(2,1)} all-gather(bf16[2,64,128]{2,1,0:T(8,128)(2,1)S(1)} %get-tuple-element.10), channel_id=1, replica_groups=mesh['sec'=4,'row'=8,'col'=32] {'row'}, dimensions={1}, use_global_device_ids=true | all-gather | bytes 294912 | tf_op jit(solution)/shard_map/all_gather | solution.py:175
  57.0 1.8 sine_convert_fusion
  58.8 1.6 fusion.204
  60.5 2.5 collective-permute-start.2
  63.0 4.6 collective-permute-start.3
  67.6 1.3 collective-permute-done.3
  69.4 1.9 collective-permute-start.4
  71.4 5.8 %collective-permute-start.5 = (bf16[2,1,66,130]{3,1,2,0:T(2,128)(2,1)S(1)}, bf16[2,1,66,130]{3,1,2,0:T(2,128)(2,1)S(1)}, u32[]{:S(2)}, u32[]{:S(2)}) collective-permute-start(bf16[2,1,66,130]{3,1,2,0:T(2,128)(2,1)S(1)} %get-tuple-element.96), channel_id=1, source_target_pairs={{1,0},{2,1},{3,2},{4,3},{5,4},{6,5},{7,6},{8,7},{9,8},{10,9},{11,1... | collective-permute-start | bytes 102968 | tf_op jit(solution)/shard_map/ppermute | solution.py:44
  77.7 57.8 %scatter_custom_fusion.1 = f32[256]{0:T(256)} fusion(s32[8192]{0:T(1024)} %bitcast.675, f32[8192]{0:T(1024)S(1)} %broadcast.90, f32[]{:T(128)} %constant.18.clone.1), kind=kCustom, calls=%fused_computation.640 | custom fusion | flops 8192 | bytes 1536 | tf_op jit(solution)/shard_map/scatter-add | solution.py:187
  144.1 3.5 collective-permute-start.6
  152.8 3.8 collective-permute-start.7
  158.8 7.8 %collective-permute-start.9 = (f32[10,2,64,1]{2,1,3,0:T(2,128)S(1)}, f32[10,2,64,1]{2,1,3,0:T(2,128)S(1)}, u32[]{:S(2)}, u32[]{:S(2)}) collective-permute-start(f32[10,2,64,1]{2,1,3,0:T(2,128)S(1)} %constant_dynamic-update-slice_fusion.30), channel_id=1, source_target_pairs={{256,0},{512,256},{768,512},{0,768},{257,1},{513,257},{769,513},{1... | collective-permute-start | bytes 15368 | tf_op jit(solution)/shard_map/ppermute | solution.py:44
  167.1 1.9 collective-permute-start.8
  180.6 2.1 collective-permute-start.10
  184.4 5.8 %collective-permute-start.11 = (bf16[10,1,64,128]{3,2,1,0:T(8,128)(2,1)S(1)}, bf16[10,1,64,128]{3,2,1,0:T(8,128)(2,1)S(1)}, u32[]{:S(2)}, u32[]{:S(2)}) collective-permute-start(bf16[10,1,64,128]{3,2,1,0:T(8,128)(2,1)S(1)} %constant_dynamic-update-slice_fusion.50), channel_id=1, source_target_pairs={{1,0},{2,1},{3,2},{4,3},{5,4},{6,5},{7,6},{8,7},{9,8},{10,9},{11,1... | collective-permute-start | bytes 491528 | tf_op jit(solution)/shard_map/ppermute | solution.py:44
  190.5 1.6 constant_dynamic-update-slice_fusion.94
  198.4 1.4 constant_dynamic-update-slice_fusion.92
  199.8 1.4 constant_dynamic-update-slice_fusion.91
  221.7 1.5 fusion
  223.6 2.6 copy.761
  226.2 44.3 %scatter_custom_fusion = f32[256,2]{1,0:T(8,128)S(1)} fusion(s32[8192]{0:T(1024)} %bitcast.676, f32[8192,2]{1,0:T(8,128)} %bitcast.639, f32[]{:T(128)} %constant.18.clone.1), kind=kCustom, calls=%fused_computation.480 | custom fusion | flops 16384 | bytes 2560 | tf_op jit(solution)/shard_map/scatter-add | solution.py:184
  270.6 190.3 %all-reduce = (f32[256,2]{1,0:T(8,128)S(1)}, f32[256]{0:T(256)S(1)}) all-reduce(f32[256,2]{1,0:T(8,128)S(1)} %scatter_custom_fusion, f32[256]{0:T(256)S(1)} %copy-done.15), channel_id=1, replica_groups=mesh['sec'=4,'row'=8,'col'=32] {'sec','row'}, use_global_device_ids=true, to_apply=%region_1.2 | all-reduce | flops 768 | bytes 6144 | tf_op jit(solution)/shard_map/psum | solution.py:190
  (301 shorter events, 60.2 us)
Async XLA Ops:
  7.2 214.6 %all-gather.2.cloned.1.call-start = ((), (), s32[]{:S(2)}) async-start(), calls=%async_computation | async-start | bytes 1310720 | tf_op jit(solution)/shard_map/all_gather | solution.py:176
  9.3 51.2 %collective-permute-start = (bf16[2,2,64,1]{3,1,2,0:T(2,128)(2,1)S(1)}, bf16[2,2,64,1]{3,1,2,0:T(2,128)(2,1)S(1)}, u32[]{:S(2)}, u32[]{:S(2)}) collective-permute-start(bf16[2,2,64,1]{3,1,2,0:T(2,128)(2,1)S(1)} %get-tuple-element.111), channel_id=1, source_target_pairs={{0,256},{256,512},{512,768},{768,0},{1,257},{257,513},{513,769},{7... | collective-permute-start | bytes 1544 | tf_op jit(solution)/shard_map/ppermute | solution.py:41
  20.2 40.2 %collective-permute-start.1 = (bf16[2,2,64,1]{3,1,2,0:T(2,128)(2,1)S(1)}, bf16[2,2,64,1]{3,1,2,0:T(2,128)(2,1)S(1)}, u32[]{:S(2)}, u32[]{:S(2)}) collective-permute-start(bf16[2,2,64,1]{3,1,2,0:T(2,128)(2,1)S(1)} %get-tuple-element.112), channel_id=1, source_target_pairs={{256,0},{512,256},{768,512},{0,768},{257,1},{513,257},{769,513},{1... | collective-permute-start | bytes 1544 | tf_op jit(solution)/shard_map/ppermute | solution.py:44
  60.5 7.1 %collective-permute-start.2 = (bf16[2,2,1,130]{3,1,2,0:T(2,128)(2,1)S(1)}, bf16[2,2,1,130]{3,1,2,0:T(2,128)(2,1)S(1)}, u32[]{:S(2)}, u32[]{:S(2)}) collective-permute-start(bf16[2,2,1,130]{3,1,2,0:T(2,128)(2,1)S(1)} %get-tuple-element.93), channel_id=1, source_target_pairs={{0,32},{32,64},{64,96},{96,128},{128,160},{160,192},{192,224},{224... | collective-permute-start | bytes 3128 | tf_op jit(solution)/shard_map/ppermute | solution.py:41
  63.0 5.9 %collective-permute-start.3 = (bf16[2,2,1,130]{3,1,2,0:T(2,128)(2,1)S(1)}, bf16[2,2,1,130]{3,1,2,0:T(2,128)(2,1)S(1)}, u32[]{:S(2)}, u32[]{:S(2)}) collective-permute-start(bf16[2,2,1,130]{3,1,2,0:T(2,128)(2,1)S(1)} %get-tuple-element.94), channel_id=1, source_target_pairs={{32,0},{64,32},{96,64},{128,96},{160,128},{192,160},{224,192},{0,2... | collective-permute-start | bytes 3128 | tf_op jit(solution)/shard_map/ppermute | solution.py:44
  69.4 66.1 %collective-permute-start.4 = (bf16[2,1,66,130]{3,1,2,0:T(2,128)(2,1)S(1)}, bf16[2,1,66,130]{3,1,2,0:T(2,128)(2,1)S(1)}, u32[]{:S(2)}, u32[]{:S(2)}) collective-permute-start(bf16[2,1,66,130]{3,1,2,0:T(2,128)(2,1)S(1)} %get-tuple-element.95), channel_id=1, source_target_pairs={{0,1},{1,2},{2,3},{3,4},{4,5},{5,6},{6,7},{7,8},{8,9},{9,10},{10,1... | collective-permute-start | bytes 102968 | tf_op jit(solution)/shard_map/ppermute | solution.py:41
  71.4 64.1 %collective-permute-start.5 = (bf16[2,1,66,130]{3,1,2,0:T(2,128)(2,1)S(1)}, bf16[2,1,66,130]{3,1,2,0:T(2,128)(2,1)S(1)}, u32[]{:S(2)}, u32[]{:S(2)}) collective-permute-start(bf16[2,1,66,130]{3,1,2,0:T(2,128)(2,1)S(1)} %get-tuple-element.96), channel_id=1, source_target_pairs={{1,0},{2,1},{3,2},{4,3},{5,4},{6,5},{7,6},{8,7},{9,8},{10,9},{11,1... | collective-permute-start | bytes 102968 | tf_op jit(solution)/shard_map/ppermute | solution.py:44
  144.1 12.5 %collective-permute-start.6 = (f32[10,2,1,128]{3,1,2,0:T(2,128)S(1)}, f32[10,2,1,128]{3,1,2,0:T(2,128)S(1)}, u32[]{:S(2)}, u32[]{:S(2)}) collective-permute-start(f32[10,2,1,128]{3,1,2,0:T(2,128)S(1)} %constant_dynamic-update-slice_fusion), channel_id=1, source_target_pairs={{0,32},{32,64},{64,96},{96,128},{128,160},{160,192},{192,224},{224... | collective-permute-start | bytes 30728 | tf_op jit(solution)/shard_map/ppermute | solution.py:41
  152.8 5.6 %collective-permute-start.7 = (f32[10,2,1,128]{3,1,2,0:T(2,128)S(1)}, f32[10,2,1,128]{3,1,2,0:T(2,128)S(1)}, u32[]{:S(2)}, u32[]{:S(2)}) collective-permute-start(f32[10,2,1,128]{3,1,2,0:T(2,128)S(1)} %constant_dynamic-update-slice_fusion.10), channel_id=1, source_target_pairs={{32,0},{64,32},{96,64},{128,96},{160,128},{192,160},{224,192},{0,2... | collective-permute-start | bytes 30728 | tf_op jit(solution)/shard_map/ppermute | solution.py:44
  156.7 19.1 %copy-start.10 = (f32[2,1,128]{2,0,1:T(2,128)}, f32[2,1,128]{2,0,1:T(2,128)S(1)}, u32[]{:S(2)}) copy-start(f32[2,1,128]{2,0,1:T(2,128)S(1)} %get-tuple-element.147) | copy-start | bytes 3076
  158.4 17.4 %copy-start.9 = (f32[2,1,128]{2,0,1:T(2,128)}, f32[2,1,128]{2,0,1:T(2,128)S(1)}, u32[]{:S(2)}) copy-start(f32[2,1,128]{2,0,1:T(2,128)S(1)} %get-tuple-element.137) | copy-start | bytes 3076
  158.4 17.4 %copy-start.11 = (f32[2,1,128]{2,0,1:T(2,128)}, f32[2,1,128]{2,0,1:T(2,128)S(1)}, u32[]{:S(2)}) copy-start(f32[2,1,128]{2,0,1:T(2,128)S(1)} %get-tuple-element.136) | copy-start | bytes 3076
  158.4 17.4 %copy-start.12 = (f32[2,1,128]{2,0,1:T(2,128)}, f32[2,1,128]{2,0,1:T(2,128)S(1)}, u32[]{:S(2)}) copy-start(f32[2,1,128]{2,0,1:T(2,128)S(1)} %get-tuple-element.134) | copy-start | bytes 3076
  158.4 17.4 %copy-start.13 = (f32[2,1,128]{2,0,1:T(2,128)}, f32[2,1,128]{2,0,1:T(2,128)S(1)}, u32[]{:S(2)}) copy-start(f32[2,1,128]{2,0,1:T(2,128)S(1)} %get-tuple-element.135) | copy-start | bytes 3076
  158.8 14.6 %collective-permute-start.9 = (f32[10,2,64,1]{2,1,3,0:T(2,128)S(1)}, f32[10,2,64,1]{2,1,3,0:T(2,128)S(1)}, u32[]{:S(2)}, u32[]{:S(2)}) collective-permute-start(f32[10,2,64,1]{2,1,3,0:T(2,128)S(1)} %constant_dynamic-update-slice_fusion.30), channel_id=1, source_target_pairs={{256,0},{512,256},{768,512},{0,768},{257,1},{513,257},{769,513},{1... | collective-permute-start | bytes 15368 | tf_op jit(solution)/shard_map/ppermute | solution.py:44
  167.1 9.5 %collective-permute-start.8 = (f32[10,2,64,1]{2,1,3,0:T(2,128)S(1)}, f32[10,2,64,1]{2,1,3,0:T(2,128)S(1)}, u32[]{:S(2)}, u32[]{:S(2)}) collective-permute-start(f32[10,2,64,1]{2,1,3,0:T(2,128)S(1)} %constant_dynamic-update-slice_fusion.20), channel_id=1, source_target_pairs={{0,256},{256,512},{512,768},{768,0},{1,257},{257,513},{513,769},{7... | collective-permute-start | bytes 15368 | tf_op jit(solution)/shard_map/ppermute | solution.py:41
  180.6 13.7 %collective-permute-start.10 = (bf16[10,1,64,128]{3,2,1,0:T(8,128)(2,1)S(1)}, bf16[10,1,64,128]{3,2,1,0:T(8,128)(2,1)S(1)}, u32[]{:S(2)}, u32[]{:S(2)}) collective-permute-start(bf16[10,1,64,128]{3,2,1,0:T(8,128)(2,1)S(1)} %constant_dynamic-update-slice_fusion.40), channel_id=1, source_target_pairs={{0,1},{1,2},{2,3},{3,4},{4,5},{5,6},{6,7},{7,8},{8,9},{9,10},{10,1... | collective-permute-start | bytes 491528 | tf_op jit(solution)/shard_map/ppermute | solution.py:41
  184.4 9.9 %collective-permute-start.11 = (bf16[10,1,64,128]{3,2,1,0:T(8,128)(2,1)S(1)}, bf16[10,1,64,128]{3,2,1,0:T(8,128)(2,1)S(1)}, u32[]{:S(2)}, u32[]{:S(2)}) collective-permute-start(bf16[10,1,64,128]{3,2,1,0:T(8,128)(2,1)S(1)} %constant_dynamic-update-slice_fusion.50), channel_id=1, source_target_pairs={{1,0},{2,1},{3,2},{4,3},{5,4},{6,5},{7,6},{8,7},{9,8},{10,9},{11,1... | collective-permute-start | bytes 491528 | tf_op jit(solution)/shard_map/ppermute | solution.py:44
  195.9 13.4 %copy-start.3 = (f32[2,64,128]{2,0,1:T(2,128)S(1)}, f32[2,64,128]{2,0,1:T(2,128)}, u32[]{:S(2)}) copy-start(f32[2,64,128]{2,0,1:T(2,128)} %get-tuple-element.85) | copy-start | bytes 196612
  195.9 14.0 %copy-start.1 = (f32[1,2,64,128]{3,1,2,0:T(2,128)S(1)}, f32[1,2,64,128]{3,1,2,0:T(2,128)}, u32[]{:S(2)}) copy-start(f32[1,2,64,128]{3,1,2,0:T(2,128)} %maximum_bitcast_fusion.10) | copy-start | bytes 196612
  196.7 13.8 %copy-start.2 = (f32[1,2,64,128]{3,1,2,0:T(2,128)S(1)}, f32[1,2,64,128]{3,1,2,0:T(2,128)}, u32[]{:S(2)}) copy-start(f32[1,2,64,128]{3,1,2,0:T(2,128)} %maximum_bitcast_fusion.11) | copy-start | bytes 196612
  197.6 14.9 %copy-start.8 = (f32[1,64,128]{2,1,0:T(8,128)S(1)}, f32[1,64,128]{2,1,0:T(8,128)}, u32[]{:S(2)}) copy-start(f32[1,64,128]{2,1,0:T(8,128)} %slice.1226) | copy-start | bytes 98308
  197.6 15.5 %copy-start.7 = (f32[1,64,128]{2,1,0:T(8,128)S(1)}, f32[1,64,128]{2,1,0:T(8,128)}, u32[]{:S(2)}) copy-start(f32[1,64,128]{2,1,0:T(8,128)} %slice.1227) | copy-start | bytes 98308
  223.6 47.0 %copy-start.15 = (f32[256]{0:T(256)S(1)}, f32[256]{0:T(256)}, u32[]{:S(2)}) copy-start(f32[256]{0:T(256)} %scatter_custom_fusion.1) | copy-start | bytes 3076
  (5 other events, 33.3 us)
Sparse Core Ops, SparseCore 0:
  57.1 67.0 all-gather.1
where the time goes:
time: 470 us; the launch traced here: 468 us
  blocking collectives  219 us (47%)
  other arithmetic  140 us (30%)
  starting transfers between devices  58.9 us (13%)
  local copies, waits for them, and re-layouts  30.4 us (6%)
  between operations  15.4 us (3%)
    psum x1, blocking collectives, on_device(): totals, counts = lax.psum((totals, counts), ('sec', 'row'))  190 us
    scatter-add x1, other arithmetic, on_device(): jax.ops.segment_sum(jnp.ones((cell_count,), jnp.float32), flat_shells, nu...  57.8 us
    scatter-add x1, other arithmetic, on_device(): jax.ops.segment_sum(power_map.reshape(depth_z, cell_count).T, flat_shells...  44.3 us
    ppermute x6, starting transfers between devices, with_halo(): lax.ppermute(lax.slice_in_dim(block, 0, width, axis=dim), axis, backward)  36 us
    all_gather x1, blocking collectives, on_device(): rows_all = lax.all_gather(order_b, 'row', axis=1, tiled=True)  28.5 us
    ppermute x6, starting transfers between devices, with_halo(): lax.ppermute(lax.slice_in_dim(block, block.shape[dim] - width, None, axis...  22.9 us
    unnamed x105, local copies, waits for them, and re-layouts  16.7 us
    unnamed x20, other arithmetic  13.1 us
  transfers between devices with their start and end apart: 13, of which 3 were waited for; matrix products, arithmetic and copies ran while one was open for 26% of the time, Pallas kernels for 0%

commit v1 on v0

v1 whole, which is shorter than its diff:
```python
import functools
import math

import jax
import jax.numpy as jnp
import ml_dtypes
import numpy as np
from jax import lax
from jax.experimental import pallas as pl
from jax.experimental.pallas import tpu as pltpu
from jax.sharding import PartitionSpec as P

NSHELL = 256
MESH = pl.DeviceIdType.MESH

LATTICE = (
    (0, 0, 0),
    (1, 0, 0),
    (-1, 0, 0),
    (0, 1, 0),
    (0, -1, 0),
    (0, 0, 1),
    (0, 0, -1),
    (1, 1, 0),
    (-1, -1, 0),
    (1, -1, 0),
    (-1, 1, 0),
    (1, 0, 1),
    (-1, 0, -1),
    (1, 0, -1),
    (-1, 0, 1),
    (0, 1, 1),
    (0, -1, -1),
    (0, 1, -1),
    (0, -1, 1),
)
WEIGHTS = (1.0 / 3.0,) + (1.0 / 18.0,) * 6 + (1.0 / 36.0,) * 12


def trig(freq, pos, full):
    turn = (freq * pos % full).astype(np.float32) * np.float32(2.0 * math.pi / full)
    return np.cos(turn), np.sin(turn)


def x_table(rows, secs, width, full):
    per = width // secs
    freq = np.arange(full // 2)[:, None]
    cos_x, sin_x = trig(freq, np.arange(full)[None, :], full)
    imag = -sin_x
    imag[0] = trig(full // 2, np.arange(full), full)[0]
    both = np.stack([cos_x, imag], 0).reshape(2, rows // 2, secs, per, full)
    both = both.transpose(1, 2, 0, 3, 4).reshape(rows // 2, secs * 2 * per, full)
    return both.astype(ml_dtypes.bfloat16)


def y_table(full):
    cos_y, sin_y = trig(np.arange(full)[:, None], np.arange(full)[None, :], full)
    return np.concatenate([cos_y, sin_y], 1).astype(ml_dtypes.bfloat16)


def density_pair(labels, jitter_0, jitter_1):
    heavy_a = jnp.where(labels == 1, jnp.float32(1.0), jnp.float32(0.2))
    heavy_b = jnp.where(labels == 1, jnp.float32(0.2), jnp.float32(1.0))
    return heavy_a * jitter_0, heavy_b * jitter_1


def exchange_kernel(
    sizes,
    labels_ref,
    jitter_ref,
    shells_ref,
    xtab_hbm,
    ytab_hbm,
    spec_ref,
    own_ref,
    low_ref,
    high_ref,
    xtab,
    ytab,
    order_buf,
    plane_buf,
    half_send,
    half_buf,
    shell_own,
    shell_pair,
    shell_next,
    shell_send,
    shell_buf,
    ymsg,
    ybuf,
    ext,
    xsend,
    xbuf,
    zbuf,
    mask_h,
    mask_l,
    row_send,
    row_buf,
    sec_send,
    sec_buf,
    tab_sem,
    p1_send,
    p1_recv,
    p2_send,
    p2_recv,
    s1_send,
    s1_recv,
    s2_send,
    s2_recv,
    y_send,
    y_recv,
    x_send,
    x_recv,
    z_send,
    z_recv,
    ar_send,
    ar_recv,
    as_send,
    as_recv,
):
    rows, secs, cols = sizes
    depth, width_x, width_y = labels_ref.shape
    full_x, full_y = width_x * rows, width_y * secs
    per = width_x // secs
    half = rows // 2
    row, sec, col = lax.axis_index("row"), lax.axis_index("sec"), lax.axis_index("col")

    def shifted(index, step, count):
        return lax.rem(index + step + count, count)

    barrier = pltpu.get_barrier_semaphore()
    for step in range(1, rows):
        pl.semaphore_signal(
            barrier, 1, device_id={"row": shifted(row, step, rows)}, device_id_type=MESH
        )
    for step in range(1, secs):
        pl.semaphore_signal(
            barrier, 1, device_id={"sec": shifted(sec, step, secs)}, device_id_type=MESH
        )
    for step in (1, -1):
        pl.semaphore_signal(
            barrier, 1, device_id={"col": shifted(col, step, cols)}, device_id_type=MESH
        )

    block = jnp.where(row < half, row, rows - 1 - row)
    xcopy = pltpu.make_async_copy(xtab_hbm.at[block], xtab, tab_sem.at[0])
    ycopy = pltpu.make_async_copy(ytab_hbm, ytab, tab_sem.at[1])
    xcopy.start()
    ycopy.start()

    rounded = []
    for plane in range(depth):
        dens_a, dens_b = density_pair(
            labels_ref[plane], jitter_ref[0, plane], jitter_ref[1, plane]
        )
        order_buf[plane] = (dens_a - dens_b).astype(jnp.bfloat16)
        rounded.append((dens_a.astype(jnp.bfloat16), dens_b.astype(jnp.bfloat16)))
    flat = jnp.concatenate(
        [rounded[plane][part] for part in range(2) for plane in range(depth)], axis=0
    )
    pick_row = lax.broadcasted_iota(jnp.int32, (8, width_y), 0)
    pick_lane = lax.broadcasted_iota(jnp.int32, (8, width_y), 1)
    near = (pick_row < 2) & (pick_lane == pick_row)
    far = (pick_row >= 6) & (pick_lane == pick_row + (width_y - 8))
    pick = jnp.where(near | far, 1.0, 0.0).astype(jnp.bfloat16)
    ymsg[...] = lax.dot_general(
        pick, flat, (((1,), (1,)), ((), ())), preferred_element_type=jnp.float32
    )
    shell_own[...] = shells_ref[...].astype(jnp.float32).astype(jnp.bfloat16)

    pl.semaphore_wait(barrier, rows + secs)

    waits = []

    def send(src, dst, ssem, rsem, target):
        copy = pltpu.make_async_remote_copy(
            src_ref=src,
            dst_ref=dst,
            send_sem=ssem,
            recv_sem=rsem,
            device_id=target,
            device_id_type=MESH,
        )
        copy.start()
        waits.append(copy)

    def arrive(dst, ssem, rsem, axis):
        pltpu.make_async_remote_copy(
            src_ref=dst,
            dst_ref=dst,
            send_sem=ssem,
            recv_sem=rsem,
            device_id=axis,
            device_id_type=MESH,
        ).wait_recv()

    for step in range(1, rows):
        target = shifted(row, step, rows)
        send(
            order_buf.at[target // half],
            plane_buf.at[row],
            p1_send.at[step - 1],
            p1_recv.at[step - 1],
            {"row": target},
        )
    for place, step in enumerate((1, -1)):
        send(
            ymsg,
            ybuf.at[place],
            y_send.at[place],
            y_recv.at[place],
            {"sec": shifted(sec, step, secs)},
        )
    mirror = rows - 1 - row
    send(shell_own, shell_pair, s1_send.at[0], s1_recv.at[0], {"row": mirror})
    next_block = lax.rem(rows - row, half)
    next_copies = [
        pltpu.make_async_remote_copy(
            src_ref=shell_own.at[pl.ds(0, 16)],
            dst_ref=shell_next,
            send_sem=s1_send.at[1 + place],
            recv_sem=s1_recv.at[1],
            device_id={"row": target},
            device_id_type=MESH,
        )
        for place, target in enumerate((next_block, rows - 1 - next_block))
    ]

    @pl.when(row >= half)
    def _():
        for copy in next_copies:
            copy.start()

    plane_buf[row] = jnp.where(row < half, order_buf[0], order_buf[1])

    arrive(shell_pair, s1_send.at[0], s1_recv.at[0], {"row": mirror})
    arrive(shell_next, s1_send.at[1], s1_recv.at[1], {"row": mirror})
    mine = shell_own[...].astype(jnp.float32)
    other = shell_pair[...].astype(jnp.float32)
    plus = jnp.where(row < half, mine, other)
    minus = jnp.where(row < half, other, mine)
    following = shell_next[...].astype(jnp.float32)[0:1]
    row_id = lax.broadcasted_iota(jnp.int32, (width_x, width_y), 0)
    minus = jnp.where(
        row_id == width_x - 1,
        jnp.broadcast_to(following, (width_x, width_y)),
        pltpu.roll(minus, width_x - 1, 0),
    )
    for target in range(secs):
        begin = width_x - per - per * target
        shell_send[target] = jnp.concatenate(
            [plus[per * target : per * target + per], minus[begin : begin + per]], axis=0
        ).astype(jnp.bfloat16)
    for step in range(1, secs):
        target = shifted(sec, step, secs)
        send(
            shell_send.at[target],
            shell_buf.at[sec],
            s2_send.at[step - 1],
            s2_recv.at[step - 1],
            {"sec": target},
        )
    shell_buf[sec] = shell_send[sec]

    for place in range(2):
        arrive(ybuf.at[place], y_send.at[place], y_recv.at[place], {"sec": sec})
    lanes = flat.shape[0]
    side = lax.broadcasted_iota(jnp.int32, (8, lanes), 0) < 4
    columns = jnp.where(side, ybuf[1], ybuf[0])
    yhalo = lax.dot_general(
        columns.T.astype(jnp.bfloat16),
        pick,
        (((1,), (0,)), ((), ())),
        preferred_element_type=jnp.float32,
    )
    for part in range(2 * depth):
        begin = part * width_x
        ext[part, 0:width_x, 0:width_y] = flat[begin : begin + width_x].astype(jnp.float32)
        ext[part, 0:width_x, width_y : 2 * width_y] = yhalo[begin : begin + width_x]
    xsend[0] = ext[:, width_x - 8 : width_x, :]
    xsend[1] = ext[:, 0:8, :]
    for place, step in enumerate((1, -1)):
        send(
            xsend.at[place],
            xbuf.at[place],
            x_send.at[place],
            x_recv.at[place],
            {"row": shifted(row, step, rows)},
        )

    xcopy.wait()
    for step in range(1, rows):
        arrive(
            plane_buf.at[shifted(row, -step, rows)],
            p1_send.at[step - 1],
            p1_recv.at[step - 1],
            {"row": row},
        )
    half_step = jnp.dot(
        xtab[...],
        plane_buf[...].reshape(full_x, width_y),
        preferred_element_type=jnp.float32,
    )
    half_send[...] = half_step.astype(jnp.bfloat16).reshape(secs, 2 * per, width_y)
    for step in range(1, secs):
        target = shifted(sec, step, secs)
        send(
            half_send.at[target],
            half_buf.at[sec],
            p2_send.at[step - 1],
            p2_recv.at[step - 1],
            {"sec": target},
        )
    half_buf[sec] = half_send[sec]

    for place in range(2):
        arrive(xbuf.at[place], x_send.at[place], x_recv.at[place], {"row": row})
    upper = lax.broadcasted_iota(jnp.int32, (2 * depth, 8, 2 * width_y), 1) < 4
    ext[:, width_x : width_x + 8, :] = jnp.where(upper, xbuf[1], xbuf[0])
    own_ref[...] = ext[...].reshape(own_ref.shape).astype(jnp.bfloat16)
    for place, step in enumerate((1, -1)):
        send(
            own_ref,
            zbuf.at[place],
            z_send.at[place],
            z_recv.at[place],
            {"col": shifted(col, step, cols)},
        )

    for step in range(1, secs):
        arrive(
            shell_buf.at[shifted(sec, -step, secs)],
            s2_send.at[step - 1],
            s2_recv.at[step - 1],
            {"sec": sec},
        )
    shell_rows = jnp.concatenate(
        [shell_buf[source].astype(jnp.float32) for source in range(secs)], axis=1
    )
    shell_h = jnp.floor(shell_rows * (1.0 / 16.0))
    shell_l = shell_rows - 16.0 * shell_h
    label = lax.broadcasted_iota(jnp.int32, (16, full_y), 0).astype(jnp.float32)
    for line in range(2 * per):
        span = slice(line * full_y, (line + 1) * full_y)
        mask_h[:, span] = jnp.where(
            jnp.broadcast_to(shell_h[line : line + 1], (16, full_y)) == label, 1.0, 0.0
        ).astype(jnp.bfloat16)
        mask_l[32:48, span] = jnp.where(
            jnp.broadcast_to(shell_l[line : line + 1], (16, full_y)) == label, 1.0, 0.0
        ).astype(jnp.bfloat16)

    ycopy.wait()
    for step in range(1, secs):
        arrive(
            half_buf.at[shifted(sec, -step, secs)],
            p2_send.at[step - 1],
            p2_recv.at[step - 1],
            {"sec": sec},
        )
    left = jnp.concatenate([half_buf[source] for source in range(secs)], axis=1)
    product = jnp.dot(left, ytab[...], preferred_element_type=jnp.float32)
    re_cos, re_sin = product[:per, :full_y], product[:per, full_y:]
    im_cos, im_sin = product[per:, :full_y], product[per:, full_y:]
    sum_re, sum_im = re_cos + im_sin, im_cos - re_sin
    dif_re, dif_im = re_cos - im_sin, im_cos + re_sin
    first = (lax.broadcasted_iota(jnp.int32, (per, full_y), 0) == 0) & (
        (block == 0) & (sec == 0)
    )
    sum_re = jnp.where(first, re_cos, sum_re)
    sum_im = jnp.where(first, re_sin, sum_im)
    dif_re = jnp.where(first, im_cos, dif_re)
    dif_im = jnp.where(first, im_sin, dif_im)
    power = (sum_re * sum_re + sum_im * sum_im, dif_re * dif_re + dif_im * dif_im)
    coarse = [value.astype(jnp.bfloat16).astype(jnp.float32) for value in power]
    fine = [value - top for value, top in zip(power, coarse)]
    for line in range(2 * per):
        span = slice(line * full_y, (line + 1) * full_y)
        sign, kx = (0, line) if line < per else (1, 2 * per - 1 - line)
        member = mask_l[32:48, span].astype(jnp.float32)
        top = jnp.broadcast_to(coarse[sign][kx : kx + 1], (16, full_y))
        rest = jnp.broadcast_to(fine[sign][kx : kx + 1], (16, full_y))
        mask_l[0:16, span] = (member * top).astype(jnp.bfloat16)
        mask_l[16:32, span] = (member * rest).astype(jnp.bfloat16)
    table = lax.dot_general(
        mask_h[...],
        mask_l[...],
        (((1,), (1,)), ((), ())),
        preferred_element_type=jnp.float32,
    )
    row_send[...] = jnp.concatenate(
        [table, jnp.zeros((16, 128 - table.shape[1]), jnp.float32)], axis=1
    )

    for step in range(1, rows):
        send(
            row_send,
            row_buf.at[row],
            ar_send.at[step - 1],
            ar_recv.at[step - 1],
            {"row": shifted(row, step, rows)},
        )
    row_buf[row] = row_send[...]

    for place in range(2):
        arrive(zbuf.at[place], z_send.at[place], z_recv.at[place], {"col": col})
    low_ref[...] = zbuf[0]
    high_ref[...] = zbuf[1]

    for step in range(1, rows):
        arrive(
            row_buf.at[shifted(row, -step, rows)],
            ar_send.at[step - 1],
            ar_recv.at[step - 1],
            {"row": row},
        )
    total_0, total_1 = row_buf[0], row_buf[half]
    for source in range(1, half):
        total_0 = total_0 + row_buf[source]
        total_1 = total_1 + row_buf[half + source]
    sec_send[...] = total_0 + pltpu.roll(total_1, 64, 1)
    for step in range(1, secs):
        send(
            sec_send,
            sec_buf.at[sec],
            as_send.at[step - 1],
            as_recv.at[step - 1],
            {"sec": shifted(sec, step, secs)},
        )
    sec_buf[sec] = sec_send[...]
    for step in range(1, secs):
        arrive(
            sec_buf.at[shifted(sec, -step, secs)],
            as_send.at[step - 1],
            as_recv.at[step - 1],
            {"sec": sec},
        )
    total = sec_buf[0]
    for source in range(1, secs):
        total = total + sec_buf[source]
    lane = lax.broadcasted_iota(jnp.int32, (16, 128), 1)
    line_id = lax.broadcasted_iota(jnp.int32, (16, 256), 0)
    here = lax.broadcasted_iota(jnp.int32, (16, 256), 1) // 16 == line_id

    def spread(value):
        value = jnp.where(lane < 16, value, 0.0)
        for shift in (16, 32, 64):
            value = value + pltpu.roll(value, shift, 1)
        value = jnp.concatenate([value, value], axis=1)
        return jnp.sum(jnp.where(here, value, 0.0), axis=0, keepdims=True)

    both = total + pltpu.roll(total, 112, 1)
    scale = spread(pltpu.roll(total, 96, 1)) * float(full_x * full_y)
    spec_ref[0:1, :] = spread(both) / scale
    spec_ref[1:2, :] = spread(pltpu.roll(both, 64, 1)) / scale

    for copy in waits:
        copy.wait_send()

    @pl.when(row >= half)
    def _():
        for copy in next_copies:
            copy.wait_send()


def exchange(labels, jitter, shells, sizes):
    rows, secs, _ = sizes
    depth, width_x, width_y = labels.shape
    per = width_x // secs
    full_x, full_y = width_x * rows, width_y * secs
    ext_rows = 2 * depth * (width_x + 8)
    bf16, f32 = jnp.bfloat16, jnp.float32
    vmem = pl.BlockSpec(memory_space=pltpu.VMEM)
    hbm = pl.BlockSpec(memory_space=pl.ANY)
    dma = pltpu.SemaphoreType.DMA
    halo = jax.ShapeDtypeStruct((ext_rows, 2 * width_y), bf16)
    return pl.pallas_call(
        functools.partial(exchange_kernel, sizes),
        out_shape=(jax.ShapeDtypeStruct((depth, NSHELL), f32), halo, halo, halo),
        in_specs=[vmem, vmem, vmem, hbm, hbm],
        out_specs=(vmem,) * 4,
        scratch_shapes=[
            pltpu.VMEM((secs * 2 * per, full_x), bf16),
            pltpu.VMEM((full_y, 2 * full_y), bf16),
            pltpu.VMEM((depth, width_x, width_y), bf16),
            pltpu.VMEM((rows, width_x, width_y), bf16),
            pltpu.VMEM((secs, 2 * per, width_y), bf16),
            pltpu.VMEM((secs, 2 * per, width_y), bf16),
            pltpu.VMEM((width_x, width_y), bf16),
            pltpu.VMEM((width_x, width_y), bf16),
            pltpu.VMEM((16, width_y), bf16),
            pltpu.VMEM((secs, 2 * per, width_y), bf16),
            pltpu.VMEM((secs, 2 * per, width_y), bf16),
            pltpu.VMEM((8, 2 * depth * width_x), f32),
            pltpu.VMEM((2, 8, 2 * depth * width_x), f32),
            pltpu.VMEM((2 * depth, width_x + 8, 2 * width_y), f32),
            pltpu.VMEM((2, 2 * depth, 8, 2 * width_y), f32),
            pltpu.VMEM((2, 2 * depth, 8, 2 * width_y), f32),
            pltpu.VMEM((2, ext_rows, 2 * width_y), bf16),
            pltpu.VMEM((16, 2 * per * full_y), bf16),
            pltpu.VMEM((48, 2 * per * full_y), bf16),
            pltpu.VMEM((16, 128), f32),
            pltpu.VMEM((rows, 16, 128), f32),
            pltpu.VMEM((16, 128), f32),
            pltpu.VMEM((secs, 16, 128), f32),
            dma((2,)),
            dma((rows - 1,)),
            dma((rows - 1,)),
            dma((secs - 1,)),
            dma((secs - 1,)),
            dma((3,)),
            dma((2,)),
            dma((secs - 1,)),
            dma((secs - 1,)),
            dma((2,)),
            dma((2,)),
            dma((2,)),
            dma((2,)),
            dma((2,)),
            dma((2,)),
            dma((rows - 1,)),
            dma((rows - 1,)),
            dma((secs - 1,)),
            dma((secs - 1,)),
        ],
        compiler_params=pltpu.CompilerParams(collective_id=0, has_side_effects=True),
        name="exchange",
    )(
        labels,
        jitter,
        shells,
        jnp.asarray(x_table(rows, secs, width_x, full_x)),
        jnp.asarray(y_table(full_y)),
    )


def stream_kernel(labels_ref, jitter_ref, own_ref, low_ref, high_ref, out_ref, field):
    part = pl.program_id(0)
    plane = pl.program_id(1)
    depth, width_x, width_y = labels_ref.shape
    rows, lanes = field.shape[2], field.shape[3]

    @pl.when((part == 0) & (plane == 0))
    def _():
        shape = (2, depth, rows, lanes)
        field[:, 0:depth] = low_ref[...].astype(jnp.float32).reshape(shape)
        field[:, depth : 2 * depth] = own_ref[...].astype(jnp.float32).reshape(shape)
        field[:, 2 * depth : 3 * depth] = high_ref[...].astype(jnp.float32).reshape(shape)
        for level in range(depth):
            pair = density_pair(labels_ref[level], jitter_ref[0, level], jitter_ref[1, level])
            for which in range(2):
                field[which, depth + level, 0:width_x, 0:width_y] = pair[which]

    def moved(value, step, axis):
        return value if step == 0 else pltpu.roll(value, step % value.shape[axis], axis)

    other = [field[1 - part, plane + level] for level in range(5)]
    around_x = [moved(value, 1, 0) + moved(value, -1, 0) for value in other]
    around_y = [moved(value, 1, 1) + moved(value, -1, 1) for value in other]
    flat_sum = [
        2.0 * other[level] + around_x[level] + around_y[level] for level in range(5)
    ]
    for shift_z in (1, 0, -1):
        level = 2 - shift_z
        between = 2.0 * other[level] + other[level + 1] + other[level - 1]
        tall_x = between + around_y[level]
        tall_y = between + around_x[level]
        gain = -1.6 / 36.0
        vel_x = gain * (moved(tall_x, -1, 0) - moved(tall_x, 1, 0))
        vel_y = gain * (moved(tall_y, -1, 1) - moved(tall_y, 1, 1))
        vel_z = gain * (flat_sum[level + 1] - flat_sum[level - 1])
        density = field[part, plane + level]
        rest = density * (
            1.0 - 1.875 * (vel_x * vel_x + vel_y * vel_y + vel_z * vel_z)
        )
        for number, (offsets, weight) in enumerate(zip(LATTICE, WEIGHTS)):
            if offsets[2] != shift_z:
                continue
            along = None
            for step, speed in zip(offsets, (vel_x, vel_y, vel_z)):
                if step != 0:
                    term = speed if step == 1 else -speed
                    along = term if along is None else along + term
            value = rest
            if along is not None:
                value = rest + density * (along * (3.75 + 5.625 * along))
            value = weight * value
            value = moved(moved(value, offsets[0], 0), offsets[1], 1)
            out_ref[number, 0] = value[0:width_x, 0:width_y]


def stream(labels, jitter, own, low, high):
    depth, width_x, width_y = labels.shape
    vmem = pl.BlockSpec(memory_space=pltpu.VMEM)
    return pl.pallas_call(
        stream_kernel,
        grid=(2, depth),
        out_shape=jax.ShapeDtypeStruct((38, depth, width_x, width_y), jnp.float32),
        in_specs=[vmem] * 5,
        out_specs=pl.BlockSpec(
            (19, 1, width_x, width_y), lambda part, plane: (part, plane, 0, 0)
        ),
        scratch_shapes=[
            pltpu.VMEM((2, 3 * depth, width_x + 8, 2 * width_y), jnp.float32)
        ],
        name="stream",
    )(labels, jitter, own, low, high)


def solution(mesh):
    sizes = tuple(mesh.shape[name] for name in ("row", "sec", "col"))

    def on_device(labels, jitter, shells):
        spectrum, own, low, high = exchange(labels, jitter, shells, sizes)
        return stream(labels, jitter, own, low, high), spectrum

    in_specs = (P("col", "row", "sec"), P(None, "col", "row", "sec"), P("row", "sec"))
    out_specs = (P(None, "col", "row", "sec"), P("col", None))
    return jax.shard_map(
        on_device, mesh=mesh, in_specs=in_specs, out_specs=out_specs, check_vma=False
    )
```

time: 470 us -> 58.1 us (0.12)
  the two profiles are of different devices: /device:TPU:64 before, /device:TPU:2 now
where the time goes in v1:
time: 58.1 us; the launch traced here: 57.9 us
  Pallas kernels  56.7 us (98%)
  between operations  0.65 us (1%)
    pallas_call x1, Pallas kernels, exchange(): pl.pallas_call(functools.partial(exchange_kernel, sizes), out_shape=(jax....  50.9 us
    pallas_call x1, Pallas kernels, stream(): pl.pallas_call(stream_kernel, grid=(2, depth), out_shape=jax.ShapeDtypeSt...  5.78 us

profile of v1, /device:TPU:2, one launch (start us, length us, event | category | flops | bytes accessed | tf_op | source)
XLA Modules:
  0.0 57.9 jit_solution(12901580443253215976)
XLA Ops:
  0.6 50.9 %exchange.1 = (f32[2,256]{1,0:T(2,128)}, bf16[288,256]{1,0:T(8,128)(2,1)}, bf16[288,256]{1,0:T(8,128)(2,1)}, bf16[288,256]{1,0:T(8,128)(2,1)}) custom-call(s32[2,64,128]{2,1,0:T(8,128)} %labels_ref.3, f32[2,2,64,128]{3,2,1,0:T(8,128)} %jitter_ref.3, s32[64,128]{1,0:T(8,128)} %shells_ref.1, bf16[4,128,512]{2,1,0:T(8,128)(2,1)} %constant.4.clone.xtab_hbm, ...), custom_call_target="tpu_custom_call" | custom-call | tf_op jit(solution)/shard_map/exchange/pallas_call | solution.py:476
  51.5 0.0 copy-start
  51.6 5.8 %stream.1 = f32[38,2,64,128]{3,2,1,0:T(8,128)} custom-call(s32[2,64,128]{2,1,0:T(8,128)} %labels_ref.3, f32[2,2,64,128]{3,2,1,0:T(8,128)} %jitter_ref.3, bf16[288,256]{1,0:T(8,128)(2,1)} %get-tuple-element.6.own_ref, bf16[288,256]{1,0:T(8,128)(2,1)} %get-tuple-element.7.low_ref, bf16[288,256]{1,0:T(8,128)(2,1)} %get-tuple-element.8.high_ref), custom_call_target="tpu_custom_call" | custom-call | tf_op jit(solution)/shard_map/stream/pallas_call | solution.py:594
  57.3 0.0 copy-done
  57.3 0.6 copy.8
Async XLA Ops:
  51.5 5.8 %copy-start = (f32[2,256]{1,0:T(2,128)S(1)}, f32[2,256]{1,0:T(2,128)}, u32[]{:S(2)}) copy-start(f32[2,256]{1,0:T(2,128)} %get-tuple-element.13) | copy-start | bytes 6148

commit v2 on v1

v2 whole, which is shorter than its diff:
```python
import functools
import math

import jax
import jax.numpy as jnp
import ml_dtypes
import numpy as np
from jax import lax
from jax.experimental import pallas as pl
from jax.experimental.pallas import tpu as pltpu
from jax.sharding import PartitionSpec as P

NSHELL = 256
MESH = pl.DeviceIdType.MESH

LATTICE = (
    (0, 0, 0),
    (1, 0, 0),
    (-1, 0, 0),
    (0, 1, 0),
    (0, -1, 0),
    (0, 0, 1),
    (0, 0, -1),
    (1, 1, 0),
    (-1, -1, 0),
    (1, -1, 0),
    (-1, 1, 0),
    (1, 0, 1),
    (-1, 0, -1),
    (1, 0, -1),
    (-1, 0, 1),
    (0, 1, 1),
    (0, -1, -1),
    (0, 1, -1),
    (0, -1, 1),
)
WEIGHTS = (1.0 / 3.0,) + (1.0 / 18.0,) * 6 + (1.0 / 36.0,) * 12


def trig(freq, pos, full):
    turn = (freq * pos % full).astype(np.float32) * np.float32(2.0 * math.pi / full)
    return np.cos(turn), np.sin(turn)


def x_table(rows, width, full):
    cos_x, sin_x = trig(np.arange(full // 2)[:, None], np.arange(full)[None, :], full)
    imag = -sin_x
    imag[0] = trig(full // 2, np.arange(full), full)[0]
    both = np.stack([cos_x, imag], 0).reshape(2, rows // 2, width, full)
    both = both.transpose(1, 0, 2, 3).reshape(rows // 2, 2 * width, full)
    return both.astype(ml_dtypes.bfloat16)


def y_table(full):
    cos_y, sin_y = trig(np.arange(full)[:, None], np.arange(full)[None, :], full)
    return np.concatenate([cos_y, sin_y], 1).astype(ml_dtypes.bfloat16)


def density_pair(labels, jitter_0, jitter_1):
    heavy_a = jnp.where(labels == 1, jnp.float32(1.0), jnp.float32(0.2))
    heavy_b = jnp.where(labels == 1, jnp.float32(0.2), jnp.float32(1.0))
    return heavy_a * jitter_0, heavy_b * jitter_1


def populations_of(part, field, out_buf):
    _, levels, rows, lanes = field.shape
    width_x, width_y = rows - 8, lanes // 2
    depth = levels - 4
    lane = lax.broadcasted_iota(jnp.int32, (rows, width_y), 1)

    def moved(value, step, axis):
        return pltpu.roll(value, step % value.shape[axis], axis)

    def streamed(value, step_x, step_y):
        if step_y != 0:
            shift, edge = (1, 0) if step_y == 1 else (width_y - 1, width_y - 1)
            value = jnp.where(
                lane == edge,
                pltpu.roll(value[:, width_y:], shift, 1),
                pltpu.roll(value[:, :width_y], shift, 1),
            )
        if step_x != 0:
            value = moved(value, step_x, 0)
        return value[:width_x]

    other, around_x, around_y = [], [], []
    for level in range(levels):
        value = field[1 - part, level]
        other.append(value)
        around_x.append(moved(value, 1, 0) + moved(value, -1, 0))
        around_y.append(moved(value, 1, 1) + moved(value, -1, 1))
    flat_sum = [
        2.0 * other[level] + around_x[level] + around_y[level] for level in range(levels)
    ]
    gain = -1.6 / 36.0
    for level in range(1, levels - 1):
        between = 2.0 * other[level] + other[level + 1] + other[level - 1]
        tall_x = between + around_y[level]
        tall_y = between + around_x[level]
        speeds = (
            gain * (moved(tall_x, -1, 0) - moved(tall_x, 1, 0)),
            gain * (moved(tall_y, -1, 1) - moved(tall_y, 1, 1)),
            gain * (flat_sum[level + 1] - flat_sum[level - 1]),
        )
        density = field[part, level]
        squares = speeds[0] * speeds[0] + speeds[1] * speeds[1] + speeds[2] * speeds[2]
        rest = density * (1.0 - 1.875 * squares)
        scaled = {}
        for weight in sorted(set(WEIGHTS)):
            scaled[weight] = (
                weight * rest,
                (3.75 * weight) * density,
                (5.625 * weight) * density,
            )
        for number, (offsets, weight) in enumerate(zip(LATTICE, WEIGHTS)):
            target = level - 2 + offsets[2]
            if target < 0 or target >= depth:
                continue
            span = lanes if offsets[1] != 0 else width_y
            base, linear, square = (value[:, :span] for value in scaled[weight])
            along = None
            for step, speed in zip(offsets, speeds):
                if step != 0:
                    term = speed[:, :span]
                    if along is None:
                        along = term if step == 1 else -term
                    else:
                        along = along + term if step == 1 else along - term
            value = base
            if along is not None:
                value = base + along * (linear + square * along)
            out_buf[part * 19 + number, target] = streamed(value, offsets[0], offsets[1])


def exchange_kernel(
    sizes,
    labels_ref,
    jitter_ref,
    shells_ref,
    xtab_hbm,
    ytab_hbm,
    pop_hbm,
    spec_ref,
    xtab,
    ytab,
    order_buf,
    plane_buf,
    half_send,
    half_buf,
    shell_own,
    shell_pair,
    shell_next,
    shell_send,
    shell_buf,
    ymsg,
    ybuf,
    ext,
    xsend,
    xbuf,
    zsend,
    zbuf,
    field,
    out_buf,
    mask_h,
    mask_l,
    counts,
    power,
    row_send,
    row_buf,
    spec_send,
    spec_buf,
    tab_sem,
    out_sem,
    p1_send,
    p1_recv,
    p2_send,
    p2_recv,
    s1_send,
    s1_recv,
    s2_send,
    s2_recv,
    y_send,
    y_recv,
    x_send,
    x_recv,
    z_send,
    z_recv,
    ar_send,
    ar_recv,
    as_send,
    as_recv,
):
    rows, secs, cols = sizes
    depth, width_x, width_y = labels_ref.shape
    full_x, full_y = width_x * rows, width_y * secs
    half = rows // 2
    row, sec, col = lax.axis_index("row"), lax.axis_index("sec"), lax.axis_index("col")
    hub = sec == 0

    def shifted(index, step, count):
        return lax.rem(index + step + count, count)

    barrier = pltpu.get_barrier_semaphore()
    for step in range(1, rows):
        pl.semaphore_signal(
            barrier, 1, device_id={"row": shifted(row, step, rows)}, device_id_type=MESH
        )
    for step in range(1, secs):
        pl.semaphore_signal(
            barrier, 1, device_id={"sec": shifted(sec, step, secs)}, device_id_type=MESH
        )
    for step in (1, -1):
        pl.semaphore_signal(
            barrier, 1, device_id={"col": shifted(col, step, cols)}, device_id_type=MESH
        )

    block = jnp.where(row < half, row, rows - 1 - row)
    xcopy = pltpu.make_async_copy(xtab_hbm.at[block], xtab, tab_sem.at[0])
    ycopy = pltpu.make_async_copy(ytab_hbm, ytab, tab_sem.at[1])
    xcopy.start()
    ycopy.start()

    rounded = []
    for plane in range(depth):
        pair = density_pair(labels_ref[plane], jitter_ref[0, plane], jitter_ref[1, plane])
        order_buf[plane] = (pair[0] - pair[1]).astype(jnp.bfloat16)
        rounded.append([value.astype(jnp.bfloat16) for value in pair])
    flat = jnp.concatenate(
        [rounded[plane][part] for part in range(2) for plane in range(depth)], axis=0
    )
    pick_row = lax.broadcasted_iota(jnp.int32, (8, width_y), 0)
    pick_lane = lax.broadcasted_iota(jnp.int32, (8, width_y), 1)
    near = (pick_row < 2) & (pick_lane == pick_row)
    far = (pick_row >= 6) & (pick_lane == pick_row + (width_y - 8))
    pick = jnp.where(near | far, 1.0, 0.0).astype(jnp.bfloat16)
    ymsg[...] = lax.dot_general(
        pick, flat, (((1,), (1,)), ((), ())), preferred_element_type=jnp.float32
    )
    shell_own[...] = shells_ref[...].astype(jnp.float32).astype(jnp.bfloat16)

    pl.semaphore_wait(barrier, rows + secs)

    waits = []

    def transfer(src, dst, ssem, rsem, target):
        return pltpu.make_async_remote_copy(
            src_ref=src,
            dst_ref=dst,
            send_sem=ssem,
            recv_sem=rsem,
            device_id=target,
            device_id_type=MESH,
        )

    def send(src, dst, ssem, rsem, target):
        copy = transfer(src, dst, ssem, rsem, target)
        copy.start()
        waits.append(copy)

    def arrive(dst, ssem, rsem, target):
        transfer(dst, dst, ssem, rsem, target).wait_recv()

    order = sorted(range(1, rows), key=lambda step: -min(step, rows - step))
    for step in order:
        target = shifted(row, step, rows)
        send(
            order_buf.at[target // half],
            plane_buf.at[row],
            p1_send.at[step - 1],
            p1_recv.at[step - 1],
            {"row": target},
        )
    for place, step in enumerate((1, -1)):
        send(
            ymsg,
            ybuf.at[place],
            y_send.at[place],
            y_recv.at[place],
            {"sec": shifted(sec, step, secs)},
        )
    mirror = rows - 1 - row
    send(shell_own, shell_pair, s1_send.at[0], s1_recv.at[0], {"row": mirror})
    next_block = lax.rem(rows - row, half)
    next_copies = [
        transfer(
            shell_own.at[pl.ds(0, 16)],
            shell_next,
            s1_send.at[1 + place],
            s1_recv.at[1],
            {"row": target},
        )
        for place, target in enumerate((next_block, rows - 1 - next_block))
    ]

    @pl.when(row >= half)
    def _():
        for copy in next_copies:
            copy.start()

    plane_buf[row] = jnp.where(row < half, order_buf[0], order_buf[1])

    arrive(shell_pair, s1_send.at[0], s1_recv.at[0], {"row": mirror})
    arrive(shell_next, s1_send.at[1], s1_recv.at[1], {"row": mirror})
    mine = shell_own[...].astype(jnp.float32)
    paired = shell_pair[...].astype(jnp.float32)
    plus = jnp.where(row < half, mine, paired)
    minus = jnp.where(row < half, paired, mine)
    following = shell_next[...].astype(jnp.float32)[0:1]
    row_id = lax.broadcasted_iota(jnp.int32, (width_x, width_y), 0)
    minus = jnp.where(
        row_id == width_x - 1,
        jnp.broadcast_to(following, (width_x, width_y)),
        pltpu.roll(minus, width_x - 1, 0),
    )
    shell_send[...] = jnp.concatenate([plus, minus], axis=0).astype(jnp.bfloat16)
    from_sec = jnp.maximum(sec - 1, 0)
    shell_copy = transfer(
        shell_send, shell_buf.at[sec], s2_send.at[0], s2_recv.at[from_sec], {"sec": 0}
    )

    @pl.when(sec > 0)
    def _():
        shell_copy.start()

    for place in range(2):
        arrive(ybuf.at[place], y_send.at[place], y_recv.at[place], {"sec": sec})
    lanes = flat.shape[0]
    side = lax.broadcasted_iota(jnp.int32, (8, lanes), 0) < 4
    columns = jnp.where(side, ybuf[1], ybuf[0])
    yhalo = lax.dot_general(
        columns.T.astype(jnp.bfloat16),
        pick,
        (((1,), (0,)), ((), ())),
        preferred_element_type=jnp.float32,
    )
    for part in range(2 * depth):
        begin = part * width_x
        ext[part, 0:width_x, 0:width_y] = flat[begin : begin + width_x].astype(jnp.float32)
        ext[part, 0:width_x, width_y : 2 * width_y] = yhalo[begin : begin + width_x]
    xsend[0] = ext[:, width_x - 8 : width_x, :]
    xsend[1] = ext[:, 0:8, :]
    for place, step in enumerate((1, -1)):
        send(
            xsend.at[place],
            xbuf.at[place],
            x_send.at[place],
            x_recv.at[place],
            {"row": shifted(row, step, rows)},
        )

    xcopy.wait()
    for step in order:
        arrive(
            plane_buf.at[shifted(row, -step, rows)],
            p1_send.at[step - 1],
            p1_recv.at[step - 1],
            {"row": row},
        )
    half_step = jnp.dot(
        xtab[...],
        plane_buf[...].reshape(full_x, width_y),
        preferred_element_type=jnp.float32,
    )
    half_send[...] = half_step.astype(jnp.bfloat16)
    half_copy = transfer(
        half_send, half_buf.at[sec], p2_send.at[0], p2_recv.at[from_sec], {"sec": 0}
    )

    @pl.when(sec > 0)
    def _():
        half_copy.start()

    for place in range(2):
        arrive(xbuf.at[place], x_send.at[place], x_recv.at[place], {"row": row})
    upper = lax.broadcasted_iota(jnp.int32, (2 * depth, 8, 2 * width_y), 1) < 4
    ext[:, width_x : width_x + 8, :] = jnp.where(upper, xbuf[1], xbuf[0])
    zsend[...] = ext[...].reshape(zsend.shape).astype(jnp.bfloat16)
    for place, step in enumerate((1, -1)):
        send(
            zsend,
            zbuf.at[place],
            z_send.at[place],
            z_recv.at[place],
            {"col": shifted(col, step, cols)},
        )
    shape = (2, depth, width_x + 8, 2 * width_y)
    field[:, depth : 2 * depth] = ext[...].reshape(shape)
    for plane in range(depth):
        pair = density_pair(labels_ref[plane], jitter_ref[0, plane], jitter_ref[1, plane])
        for part in range(2):
            field[part, depth + plane, 0:width_x, 0:width_y] = pair[part]

    lane = lax.broadcasted_iota(jnp.int32, (16, 128), 1)
    line_id = lax.broadcasted_iota(jnp.int32, (16, 256), 0)
    here = lax.broadcasted_iota(jnp.int32, (16, 256), 1) // 16 == line_id

    def spread(value):
        value = jnp.where(lane < 16, value, 0.0)
        for shift in (16, 32, 64):
            value = value + pltpu.roll(value, shift, 1)
        value = jnp.concatenate([value, value], axis=1)
        return jnp.sum(jnp.where(here, value, 0.0), axis=0, keepdims=True)

    def widen(value):
        blank = jnp.zeros((16, 128 - value.shape[1]), jnp.float32)
        return jnp.concatenate([value, blank], axis=1)

    def contract(left, right):
        return lax.dot_general(
            left, right, (((1,), (1,)), ((), ())), preferred_element_type=jnp.float32
        )

    @pl.when(hub)
    def _():
        shell_buf[0] = shell_send[...]
        for source in range(1, secs):
            arrive(
                shell_buf.at[source],
                s2_send.at[0],
                s2_recv.at[source - 1],
                {"sec": sec},
            )
        label = lax.broadcasted_iota(jnp.int32, (16, full_y), 0).astype(jnp.float32)

        def build(step, total):
            begin = pl.multiple_of(step * 16, 16)
            value = jnp.concatenate(
                [
                    shell_buf[source, pl.ds(begin, 16), :].astype(jnp.float32)
                    for source in range(secs)
                ],
                axis=1,
            )
            upper_digit = jnp.floor(value * (1.0 / 16.0))
            lower_digit = value - 16.0 * upper_digit
            for line in range(16):
                tall = (16, full_y)
                high = jnp.where(
                    jnp.broadcast_to(upper_digit[line : line + 1], tall) == label, 1.0, 0.0
                ).astype(jnp.bfloat16)
                low = jnp.where(
                    jnp.broadcast_to(lower_digit[line : line + 1], tall) == label, 1.0, 0.0
                ).astype(jnp.bfloat16)
                mask_h[begin + line] = high
                mask_l[begin + line] = low
                total = total + contract(high, low)
            return total

        counts[...] = lax.fori_loop(
            0, 2 * width_x // 16, build, jnp.zeros((16, 16), jnp.float32)
        )

        ycopy.wait()
        half_buf[0] = half_send[...]
        for source in range(1, secs):
            arrive(
                half_buf.at[source], p2_send.at[0], p2_recv.at[source - 1], {"sec": sec}
            )
        left = jnp.concatenate([half_buf[source] for source in range(secs)], axis=1)
        product = jnp.dot(left, ytab[...], preferred_element_type=jnp.float32)
        re_cos, re_sin = product[:width_x, :full_y], product[:width_x, full_y:]
        im_cos, im_sin = product[width_x:, :full_y], product[width_x:, full_y:]
        first = (lax.broadcasted_iota(jnp.int32, (width_x, full_y), 0) == 0) & (block == 0)
        sum_re = jnp.where(first, re_cos, re_cos + im_sin)
        sum_im = jnp.where(first, re_sin, im_cos - re_sin)
        dif_re = jnp.where(first, im_cos, re_cos - im_sin)
        dif_im = jnp.where(first, im_sin, im_cos + re_sin)
        power[0] = sum_re * sum_re + sum_im * sum_im
        power[1] = dif_re * dif_re + dif_im * dif_im

        def gather(step, total):
            begin = pl.multiple_of(step * 8, 8)
            for sign in range(2):
                value = power[sign, pl.ds(begin, 8), :]
                coarse = value.astype(jnp.bfloat16).astype(jnp.float32)
                fine = value - coarse
                for line in range(8):
                    place = begin + line
                    if sign == 1:
                        place = 2 * width_x - 1 - place
                    member = mask_l[place]
                    tall = (16, full_y)
                    top = jnp.broadcast_to(coarse[line : line + 1], tall)
                    rest = jnp.broadcast_to(fine[line : line + 1], tall)
                    right = jnp.concatenate(
                        [
                            member * top.astype(jnp.bfloat16),
                            member * rest.astype(jnp.bfloat16),
                        ],
                        axis=0,
                    )
                    total = total + contract(mask_h[place], right)
            return total

        table = widen(
            lax.fori_loop(0, width_x // 8, gather, jnp.zeros((16, 32), jnp.float32))
        )
        row_send[0:1, :] = spread(table + pltpu.roll(table, 112, 1))
        row_send[1:2, :] = spread(widen(counts[...]))
        for step in order:
            transfer(
                row_send,
                row_buf.at[row],
                ar_send.at[step - 1],
                ar_recv.at[step - 1],
                {"row": shifted(row, step, rows)},
            ).start()
        row_buf[row] = row_send[...]

    for place in range(2):
        arrive(zbuf.at[place], z_send.at[place], z_recv.at[place], {"col": col})
    field[:, 0:depth] = zbuf[0].astype(jnp.float32).reshape(shape)
    field[:, 2 * depth : 3 * depth] = zbuf[1].astype(jnp.float32).reshape(shape)
    drains = [
        pltpu.make_async_copy(
            out_buf.at[pl.ds(part * 19, 19)],
            pop_hbm.at[pl.ds(part * 19, 19)],
            out_sem.at[part],
        )
        for part in range(2)
    ]
    for part in range(2):
        populations_of(part, field, out_buf)
        drains[part].start()

    @pl.when(hub)
    def _():
        for step in order:
            arrive(
                row_buf.at[shifted(row, -step, rows)],
                ar_send.at[step - 1],
                ar_recv.at[step - 1],
                {"row": row},
            )
        sums = []
        for start in (0, half):
            total = row_buf[start]
            for source in range(start + 1, start + half):
                total = total + row_buf[source]
            sums.append(total)
        scale = sums[0][1:2] * float(full_x * full_y)
        spec_send[0:1, :] = sums[0][0:1] / scale
        spec_send[1:2, :] = sums[1][0:1] / scale
        spec_copies = [
            transfer(
                spec_send, spec_buf, as_send.at[target - 1], as_recv.at[0], {"sec": target}
            )
            for target in range(1, secs)
        ]
        for copy in spec_copies:
            copy.start()
        spec_ref[...] = spec_send[...]
        for copy in spec_copies:
            copy.wait_send()
        for step in order:
            transfer(
                row_send,
                row_buf.at[row],
                ar_send.at[step - 1],
                ar_recv.at[step - 1],
                {"row": row},
            ).wait_send()

    @pl.when(sec > 0)
    def _():
        arrive(spec_buf, as_send.at[0], as_recv.at[0], {"sec": sec})
        spec_ref[...] = spec_buf[...]
        ycopy.wait()
        shell_copy.wait_send()
        half_copy.wait_send()

    for copy in waits:
        copy.wait_send()

    @pl.when(row >= half)
    def _():
        for copy in next_copies:
            copy.wait_send()

    for copy in drains:
        copy.wait()


def exchange(labels, jitter, shells, sizes):
    rows, secs, _ = sizes
    depth, width_x, width_y = labels.shape
    full_x, full_y = width_x * rows, width_y * secs
    ext_rows = 2 * depth * (width_x + 8)
    bf16, f32 = jnp.bfloat16, jnp.float32
    vmem = pl.BlockSpec(memory_space=pltpu.VMEM)
    hbm = pl.BlockSpec(memory_space=pl.ANY)
    dma = pltpu.SemaphoreType.DMA
    return pl.pallas_call(
        functools.partial(exchange_kernel, sizes),
        out_shape=(
            jax.ShapeDtypeStruct((38, depth, width_x, width_y), f32),
            jax.ShapeDtypeStruct((depth, NSHELL), f32),
        ),
        in_specs=[vmem, vmem, vmem, hbm, hbm],
        out_specs=(hbm, vmem),
        scratch_shapes=[
            pltpu.VMEM((2 * width_x, full_x), bf16),
            pltpu.VMEM((full_y, 2 * full_y), bf16),
            pltpu.VMEM((depth, width_x, width_y), bf16),
            pltpu.VMEM((rows, width_x, width_y), bf16),
            pltpu.VMEM((2 * width_x, width_y), bf16),
            pltpu.VMEM((secs, 2 * width_x, width_y), bf16),
            pltpu.VMEM((width_x, width_y), bf16),
            pltpu.VMEM((width_x, width_y), bf16),
            pltpu.VMEM((16, width_y), bf16),
            pltpu.VMEM((2 * width_x, width_y), bf16),
            pltpu.VMEM((secs, 2 * width_x, width_y), bf16),
            pltpu.VMEM((8, 2 * depth * width_x), f32),
            pltpu.VMEM((2, 8, 2 * depth * width_x), f32),
            pltpu.VMEM((2 * depth, width_x + 8, 2 * width_y), f32),
            pltpu.VMEM((2, 2 * depth, 8, 2 * width_y), f32),
            pltpu.VMEM((2, 2 * depth, 8, 2 * width_y), f32),
            pltpu.VMEM((ext_rows, 2 * width_y), bf16),
            pltpu.VMEM((2, ext_rows, 2 * width_y), bf16),
            pltpu.VMEM((2, 3 * depth, width_x + 8, 2 * width_y), f32),
            pltpu.VMEM((38, depth, width_x, width_y), f32),
            pltpu.VMEM((2 * width_x, 16, full_y), bf16),
            pltpu.VMEM((2 * width_x, 16, full_y), bf16),
            pltpu.VMEM((16, 16), f32),
            pltpu.VMEM((2, width_x, full_y), f32),
            pltpu.VMEM((2, NSHELL), f32),
            pltpu.VMEM((rows, 2, NSHELL), f32),
            pltpu.VMEM((2, NSHELL), f32),
            pltpu.VMEM((2, NSHELL), f32),
            dma((2,)),
            dma((2,)),
            dma((rows - 1,)),
            dma((rows - 1,)),
            dma((1,)),
            dma((secs - 1,)),
            dma((3,)),
            dma((2,)),
            dma((1,)),
            dma((secs - 1,)),
            dma((2,)),
            dma((2,)),
            dma((2,)),
            dma((2,)),
            dma((2,)),
            dma((2,)),
            dma((rows - 1,)),
            dma((rows - 1,)),
            dma((secs - 1,)),
            dma((1,)),
        ],
        compiler_params=pltpu.CompilerParams(collective_id=0, has_side_effects=True),
        name="exchange",
    )(
        labels,
        jitter,
        shells,
        jnp.asarray(x_table(rows, width_x, full_x)),
        jnp.asarray(y_table(full_y)),
    )


def solution(mesh):
    sizes = tuple(mesh.shape[name] for name in ("row", "sec", "col"))

    def on_device(labels, jitter, shells):
        return exchange(labels, jitter, shells, sizes)

    in_specs = (P("col", "row", "sec"), P(None, "col", "row", "sec"), P("row", "sec"))
    out_specs = (P(None, "col", "row", "sec"), P("col", None))
    return jax.shard_map(
        on_device, mesh=mesh, in_specs=in_specs, out_specs=out_specs, check_vma=False
    )
```

time: 58.1 us -> 56 us (0.964)
  Pallas kernels: 56.7 us -> 51.1 us
  local copies, waits for them, and re-layouts: 0.58 us -> 4.04 us
    pallas_call x1 -> x0, Pallas kernels: 5.78 us -> none  [stream(): pl.pallas_call(stream_kernel, grid=(2, depth), out_shape=jax.ShapeDtypeSt...]
    unnamed x3 -> x4, local copies, waits for them, and re-layouts: 0.58 us -> 4.04 us
where the time goes in v2:
time: 56 us; the launch traced here: 55.8 us
  Pallas kernels  51.1 us (91%)
  local copies, waits for them, and re-layouts  4.04 us (7%)
  between operations  0.65 us (1%)
    pallas_call x1, Pallas kernels, exchange(): pl.pallas_call(functools.partial(exchange_kernel, sizes), out_shape=(jax....  51.1 us
    unnamed x4, local copies, waits for them, and re-layouts  4.04 us

profile of v2, /device:TPU:2, one launch (start us, length us, event | category | flops | bytes accessed | tf_op | source)
XLA Modules:
  0.0 55.8 jit_solution(9276997664497242065)
XLA Ops:
  0.6 51.1 %exchange.1 = (f32[38,2,64,128]{3,2,1,0:T(8,128)}, f32[2,256]{1,0:T(2,128)}) custom-call(s32[2,64,128]{2,1,0:T(8,128)} %labels_ref.1, f32[2,2,64,128]{3,2,1,0:T(8,128)} %jitter_ref.1, s32[64,128]{1,0:T(8,128)} %shells_ref.1, bf16[4,128,512]{2,1,0:T(8,128)(2,1)} %constant.4.clone.xtab_hbm, bf16[512,1024]{1,0:T(8,128)(2,1)} %constant.5.clone.ytab_hbm), custom_call_target="tpu_custom_call" | custom-call | tf_op jit(solution)/shard_map/exchange/pallas_call | solution.py:593
  51.7 0.0 copy-start
  51.8 3.5 %copy.9 = f32[38,2,64,128]{3,2,1,0:T(8,128)} copy(f32[38,2,64,128]{3,2,1,0:T(8,128)} %get-tuple-element.4) | data formatting | bytes 4980736
  55.2 0.0 copy-done
  55.2 0.6 %copy.10 = f32[2,256]{1,0:T(2,128)} copy(f32[2,256]{1,0:T(2,128)S(1)} %copy-done) | data formatting | bytes 4096
Async XLA Ops:
  51.7 3.5 %copy-start = (f32[2,256]{1,0:T(2,128)S(1)}, f32[2,256]{1,0:T(2,128)}, u32[]{:S(2)}) copy-start(f32[2,256]{1,0:T(2,128)} %get-tuple-element.5) | copy-start | bytes 6148

commit v3 on v2

--- a/solution.py
+++ b/solution.py
@@ -139,7 +139,7 @@
     shells_ref,
     xtab_hbm,
     ytab_hbm,
-    pop_hbm,
+    pop_ref,
     spec_ref,
     xtab,
     ytab,
@@ -148,10 +148,11 @@
     half_send,
     half_buf,
     shell_own,
+    shell_rows,
+    shell_head,
     shell_pair,
     shell_next,
-    shell_send,
-    shell_buf,
+    shells_all,
     ymsg,
     ybuf,
     ext,
@@ -159,10 +160,12 @@
     xbuf,
     zsend,
     zbuf,
+    zcol,
+    zcol_buf,
     field,
-    out_buf,
     mask_h,
     mask_l,
+    weighted,
     counts,
     power,
     row_send,
@@ -170,7 +173,6 @@
     spec_send,
     spec_buf,
     tab_sem,
-    out_sem,
     p1_send,
     p1_recv,
     p2_send,
@@ -260,6 +262,15 @@
     def arrive(dst, ssem, rsem, target):
         transfer(dst, dst, ssem, rsem, target).wait_recv()
 
+    from_sec = jnp.maximum(sec - 1, 0)
+    shell_copy = transfer(
+        shell_own, shell_rows.at[sec], s2_send.at[0], s2_recv.at[from_sec], {"sec": 0}
+    )
+
+    @pl.when(sec > 0)
+    def _():
+        shell_copy.start()
+
     order = sorted(range(1, rows), key=lambda step: -min(step, rows - step))
     for step in order:
         target = shifted(row, step, rows)
@@ -278,49 +289,7 @@
             y_recv.at[place],
             {"sec": shifted(sec, step, secs)},
         )
-    mirror = rows - 1 - row
-    send(shell_own, shell_pair, s1_send.at[0], s1_recv.at[0], {"row": mirror})
-    next_block = lax.rem(rows - row, half)
-    next_copies = [
-        transfer(
-            shell_own.at[pl.ds(0, 16)],
-            shell_next,
-            s1_send.at[1 + place],
-            s1_recv.at[1],
-            {"row": target},
-        )
-        for place, target in enumerate((next_block, rows - 1 - next_block))
-    ]
-
-    @pl.when(row >= half)
-    def _():
-        for copy in next_copies:
-            copy.start()
-
     plane_buf[row] = jnp.where(row < half, order_buf[0], order_buf[1])
-
-    arrive(shell_pair, s1_send.at[0], s1_recv.at[0], {"row": mirror})
-    arrive(shell_next, s1_send.at[1], s1_recv.at[1], {"row": mirror})
-    mine = shell_own[...].astype(jnp.float32)
-    paired = shell_pair[...].astype(jnp.float32)
-    plus = jnp.where(row < half, mine, paired)
-    minus = jnp.where(row < half, paired, mine)
-    following = shell_next[...].astype(jnp.float32)[0:1]
-    row_id = lax.broadcasted_iota(jnp.int32, (width_x, width_y), 0)
-    minus = jnp.where(
-        row_id == width_x - 1,
-        jnp.broadcast_to(following, (width_x, width_y)),
-        pltpu.roll(minus, width_x - 1, 0),
-    )
-    shell_send[...] = jnp.concatenate([plus, minus], axis=0).astype(jnp.bfloat16)
-    from_sec = jnp.maximum(sec - 1, 0)
-    shell_copy = transfer(
-        shell_send, shell_buf.at[sec], s2_send.at[0], s2_recv.at[from_sec], {"sec": 0}
-    )
-
-    @pl.when(sec > 0)
-    def _():
-        shell_copy.start()
 
     for place in range(2):
         arrive(ybuf.at[place], y_send.at[place], y_recv.at[place], {"sec": sec})
@@ -348,6 +317,35 @@
             {"row": shifted(row, step, rows)},
         )
 
+    mirror = rows - 1 - row
+    next_block = lax.rem(rows - row, half)
+    pair_copy = transfer(
+        shell_rows, shell_pair, s1_send.at[0], s1_recv.at[0], {"row": mirror}
+    )
+    next_copies = [
+        transfer(
+            shell_head,
+            shell_next,
+            s1_send.at[1 + place],
+            s1_recv.at[1],
+            {"row": target},
+        )
+        for place, target in enumerate((next_block, rows - 1 - next_block))
+    ]
+
+    @pl.when(hub)
+    def _():
+        shell_rows[0] = shell_own[...]
+        for source in range(1, secs):
+            arrive(shell_rows.at[source], s2_send.at[0], s2_recv.at[source - 1], {"sec": sec})
+        shell_head[...] = shell_rows[:, 0:16, :]
+        pair_copy.start()
+
+        @pl.when(row >= half)
+        def _():
+            for copy in next_copies:
+                copy.start()
+
     xcopy.wait()
     for step in order:
         arrive(
@@ -374,14 +372,20 @@
         arrive(xbuf.at[place], x_send.at[place], x_recv.at[place], {"row": row})
     upper = lax.broadcasted_iota(jnp.int32, (2 * depth, 8, 2 * width_y), 1) < 4
     ext[:, width_x : width_x + 8, :] = jnp.where(upper, xbuf[1], xbuf[0])
-    zsend[...] = ext[...].reshape(zsend.shape).astype(jnp.bfloat16)
+    zsend[...] = ext[:, :, 0:width_y].reshape(zsend.shape).astype(jnp.bfloat16)
+    margin = ext[:, :, width_y : 2 * width_y].reshape(zsend.shape).astype(jnp.bfloat16)
+    blank = jnp.zeros((zcol.shape[1] - margin.shape[0], width_y), jnp.bfloat16)
+    zcol[...] = lax.dot_general(
+        pick,
+        jnp.concatenate([margin, blank], axis=0),
+        (((1,), (1,)), ((), ())),
+        preferred_element_type=jnp.float32,
+    )
     for place, step in enumerate((1, -1)):
+        neighbour = {"col": shifted(col, step, cols)}
+        send(zsend, zbuf.at[place], z_send.at[place], z_recv.at[place], neighbour)
         send(
-            zsend,
-            zbuf.at[place],
-            z_send.at[place],
-            z_recv.at[place],
-            {"col": shifted(col, step, cols)},
+            zcol, zcol_buf.at[place], z_send.at[2 + place], z_recv.at[2 + place], neighbour
         )
     shape = (2, depth, width_x + 8, 2 * width_y)
     field[:, depth : 2 * depth] = ext[...].reshape(shape)
@@ -412,42 +416,45 @@
 
     @pl.when(hub)
     def _():
-        shell_buf[0] = shell_send[...]
-        for source in range(1, secs):
-            arrive(
-                shell_buf.at[source],
-                s2_send.at[0],
-                s2_recv.at[source - 1],
-                {"sec": sec},
+        arrive(shell_pair, s1_send.at[0], s1_recv.at[0], {"row": mirror})
+        arrive(shell_next, s1_send.at[1], s1_recv.at[1], {"row": mirror})
+
+        def joined(ref):
+            return jnp.concatenate(
+                [ref[source].astype(jnp.float32) for source in range(secs)], axis=1
             )
-        label = lax.broadcasted_iota(jnp.int32, (16, full_y), 0).astype(jnp.float32)
+
+        mine, paired = joined(shell_rows), joined(shell_pair)
+        minus = jnp.where(row < half, paired, mine)
+        following = jnp.broadcast_to(joined(shell_next)[0:1], minus.shape)
+        row_id = lax.broadcasted_iota(jnp.int32, minus.shape, 0)
+        shells_all[0:width_x, :] = jnp.where(row < half, mine, paired)
+        shells_all[width_x : 2 * width_x, :] = jnp.where(
+            row_id == width_x - 1, following, pltpu.roll(minus, width_x - 1, 0)
+        )
+        tall = (16, full_y)
+        label = lax.broadcasted_iota(jnp.int32, tall, 0).astype(jnp.float32)
+        chunk = 8 * full_y
+
+        def one_hot(digit):
+            return jnp.where(jnp.broadcast_to(digit, tall) == label, 1.0, 0.0).astype(
+                jnp.bfloat16
+            )
 
         def build(step, total):
-            begin = pl.multiple_of(step * 16, 16)
-            value = jnp.concatenate(
-                [
-                    shell_buf[source, pl.ds(begin, 16), :].astype(jnp.float32)
-                    for source in range(secs)
-                ],
-                axis=1,
-            )
+            value = shells_all[pl.ds(pl.multiple_of(step * 8, 8), 8), :]
             upper_digit = jnp.floor(value * (1.0 / 16.0))
             lower_digit = value - 16.0 * upper_digit
-            for line in range(16):
-                tall = (16, full_y)
-                high = jnp.where(
-                    jnp.broadcast_to(upper_digit[line : line + 1], tall) == label, 1.0, 0.0
-                ).astype(jnp.bfloat16)
-                low = jnp.where(
-                    jnp.broadcast_to(lower_digit[line : line + 1], tall) == label, 1.0, 0.0
-                ).astype(jnp.bfloat16)
-                mask_h[begin + line] = high
-                mask_l[begin + line] = low
-                total = total + contract(high, low)
-            return total
+            begin = pl.multiple_of(step * chunk, chunk)
+            for line in range(8):
+                span = pl.ds(begin + line * full_y, full_y)
+                mask_h[:, span] = one_hot(upper_digit[line : line + 1])
+                mask_l[:, span] = one_hot(lower_digit[line : line + 1])
+            span = pl.ds(begin, chunk)
+            return total + contract(mask_h[:, span], mask_l[:, span])
 
         counts[...] = lax.fori_loop(
-            0, 2 * width_x // 16, build, jnp.zeros((16, 16), jnp.float32)
+            0, 2 * width_x // 8, build, jnp.zeros((16, 16), jnp.float32)
         )
 
         ycopy.wait()
@@ -469,27 +476,22 @@
         power[1] = dif_re * dif_re + dif_im * dif_im
 
         def gather(step, total):
-            begin = pl.multiple_of(step * 8, 8)
             for sign in range(2):
-                value = power[sign, pl.ds(begin, 8), :]
+                value = power[sign, pl.ds(pl.multiple_of(step * 8, 8), 8), :]
                 coarse = value.astype(jnp.bfloat16).astype(jnp.float32)
                 fine = value - coarse
+                place = step if sign == 0 else 2 * width_x // 8 - 1 - step
+                begin = pl.multiple_of(place * chunk, chunk)
                 for line in range(8):
-                    place = begin + line
-                    if sign == 1:
-                        place = 2 * width_x - 1 - place
-                    member = mask_l[place]
-                    tall = (16, full_y)
-                    top = jnp.broadcast_to(coarse[line : line + 1], tall)
-                    rest = jnp.broadcast_to(fine[line : line + 1], tall)
-                    right = jnp.concatenate(
-                        [
-                            member * top.astype(jnp.bfloat16),
-                            member * rest.astype(jnp.bfloat16),
-                        ],
-                        axis=0,
-                    )
-                    total = total + contract(mask_h[place], right)
+                    slot = line if sign == 0 else 7 - line
+                    member = mask_l[:, pl.ds(begin + slot * full_y, full_y)]
+                    span = slice(slot * full_y, (slot + 1) * full_y)
+                    for half_id, part in enumerate((coarse, fine)):
+                        line_value = jnp.broadcast_to(part[line : line + 1], tall)
+                        weighted[sign, 16 * half_id : 16 * half_id + 16, span] = (
+                            member * line_value.astype(jnp.bfloat16)
+                        )
+                total = total + contract(mask_h[:, pl.ds(begin, chunk)], weighted[sign])
             return total
 
         table = widen(
@@ -507,21 +509,24 @@
             ).start()
         row_buf[row] = row_send[...]
 
-    for place in range(2):
+    for place, begin in enumerate((0, 2 * depth)):
         arrive(zbuf.at[place], z_send.at[place], z_recv.at[place], {"col": col})
-    field[:, 0:depth] = zbuf[0].astype(jnp.float32).reshape(shape)
-    field[:, 2 * depth : 3 * depth] = zbuf[1].astype(jnp.float32).reshape(shape)
-    drains = [
-        pltpu.make_async_copy(
-            out_buf.at[pl.ds(part * 19, 19)],
-            pop_hbm.at[pl.ds(part * 19, 19)],
-            out_sem.at[part],
-        )
-        for part in range(2)
-    ]
+        arrive(
+            zcol_buf.at[place], z_send.at[2 + place], z_recv.at[2 + place], {"col": col}
+        )
+        side_shape = (2, depth, width_x + 8, width_y)
+        margin = lax.dot_general(
+            zcol_buf[place].T.astype(jnp.bfloat16),
+            pick,
+            (((1,), (0,)), ((), ())),
+            preferred_element_type=jnp.float32,
+        )[: zsend.shape[0]]
+        field[:, begin : begin + depth, :, 0:width_y] = (
+            zbuf[place].astype(jnp.float32).reshape(side_shape)
+        )
+        field[:, begin : begin + depth, :, width_y : 2 * width_y] = margin.reshape(side_shape)
     for part in range(2):
-        populations_of(part, field, out_buf)
-        drains[part].start()
+        populations_of(part, field, pop_ref)
 
     @pl.when(hub)
     def _():
@@ -552,6 +557,13 @@
         spec_ref[...] = spec_send[...]
         for copy in spec_copies:
             copy.wait_send()
+        pair_copy.wait_send()
+
+        @pl.when(row >= half)
+        def _():
+            for copy in next_copies:
+                copy.wait_send()
+
         for step in order:
             transfer(
                 row_send,
@@ -572,20 +584,13 @@
     for copy in waits:
         copy.wait_send()
 
-    @pl.when(row >= half)
-    def _():
-        for copy in next_copies:
-            copy.wait_send()
-
-    for copy in drains:
-        copy.wait()
-
 
 def exchange(labels, jitter, shells, sizes):
     rows, secs, _ = sizes
     depth, width_x, width_y = labels.shape
     full_x, full_y = width_x * rows, width_y * secs
     ext_rows = 2 * depth * (width_x + 8)
+    col_lanes = -(-ext_rows // 128) * 128
     bf16, f32 = jnp.bfloat16, jnp.float32
     vmem = pl.BlockSpec(memory_space=pltpu.VMEM)
     hbm = pl.BlockSpec(memory_space=pl.ANY)
@@ -593,11 +598,11 @@
     return pl.pallas_call(
         functools.partial(exchange_kernel, sizes),
         out_shape=(
-            jax.ShapeDtypeStruct((38, depth, width_x, width_y), f32),
-            jax.ShapeDtypeStruct((depth, NSHELL), f32),
+            pltpu.VMEM((38, depth, width_x, width_y), f32),
+            pltpu.VMEM((depth, NSHELL), f32),
         ),
         in_specs=[vmem, vmem, vmem, hbm, hbm],
-        out_specs=(hbm, vmem),
+        out_specs=(vmem, vmem),
         scratch_shapes=[
             pltpu.VMEM((2 * width_x, full_x), bf16),
             pltpu.VMEM((full_y, 2 * full_y), bf16),
@@ -606,28 +611,30 @@
             pltpu.VMEM((2 * width_x, width_y), bf16),
             pltpu.VMEM((secs, 2 * width_x, width_y), bf16),
             pltpu.VMEM((width_x, width_y), bf16),
-            pltpu.VMEM((width_x, width_y), bf16),
-            pltpu.VMEM((16, width_y), bf16),
-            pltpu.VMEM((2 * width_x, width_y), bf16),
-            pltpu.VMEM((secs, 2 * width_x, width_y), bf16),
+            pltpu.VMEM((secs, width_x, width_y), bf16),
+            pltpu.VMEM((secs, 16, width_y), bf16),
+            pltpu.VMEM((secs, width_x, width_y), bf16),
+            pltpu.VMEM((secs, 16, width_y), bf16),
+            pltpu.VMEM((2 * width_x, full_y), f32),
             pltpu.VMEM((8, 2 * depth * width_x), f32),
             pltpu.VMEM((2, 8, 2 * depth * width_x), f32),
             pltpu.VMEM((2 * depth, width_x + 8, 2 * width_y), f32),
             pltpu.VMEM((2, 2 * depth, 8, 2 * width_y), f32),
             pltpu.VMEM((2, 2 * depth, 8, 2 * width_y), f32),
-            pltpu.VMEM((ext_rows, 2 * width_y), bf16),
-            pltpu.VMEM((2, ext_rows, 2 * width_y), bf16),
+            pltpu.VMEM((ext_rows, width_y), bf16),
+            pltpu.VMEM((2, ext_rows, width_y), bf16),
+            pltpu.VMEM((8, col_lanes), f32),
+            pltpu.VMEM((2, 8, col_lanes), f32),
             pltpu.VMEM((2, 3 * depth, width_x + 8, 2 * width_y), f32),
-            pltpu.VMEM((38, depth, width_x, width_y), f32),
-            pltpu.VMEM((2 * width_x, 16, full_y), bf16),
-            pltpu.VMEM((2 * width_x, 16, full_y), bf16),
+            pltpu.VMEM((16, 2 * width_x * full_y), bf16),
+            pltpu.VMEM((16, 2 * width_x * full_y), bf16),
+            pltpu.VMEM((2, 32, 8 * full_y), bf16),
             pltpu.VMEM((16, 16), f32),
             pltpu.VMEM((2, width_x, full_y), f32),
             pltpu.VMEM((2, NSHELL), f32),
             pltpu.VMEM((rows, 2, NSHELL), f32),
             pltpu.VMEM((2, NSHELL), f32),
             pltpu.VMEM((2, NSHELL), f32),
-            dma((2,)),
             dma((2,)),
             dma((rows - 1,)),
             dma((rows - 1,)),
@@ -641,8 +648,8 @@
             dma((2,)),
             dma((2,)),
             dma((2,)),
-            dma((2,)),
-            dma((2,)),
+            dma((4,)),
+            dma((4,)),
             dma((rows - 1,)),
             dma((rows - 1,)),
             dma((secs - 1,)),

time: 56 us -> 48.2 us (0.86)
  the two profiles are of different devices: /device:TPU:2 before, /device:TPU:4 now
where the time goes in v3:
time: 48.2 us; the launch traced here: 48 us
  Pallas kernels  45.3 us (94%)
  local copies, waits for them, and re-layouts  2.03 us (4%)
  between operations  0.64 us (1%)
    pallas_call x1, Pallas kernels, exchange(): pl.pallas_call(functools.partial(exchange_kernel, sizes), out_shape=(pltp...  45.3 us
    unnamed x2, local copies, waits for them, and re-layouts  2.03 us

profile of v3, /device:TPU:4, one launch (start us, length us, event | category | flops | bytes accessed | tf_op | source)
XLA Modules:
  0.0 48.0 jit_solution(3949440837943626549)
XLA Ops:
  0.6 45.3 %exchange.1 = (f32[38,2,64,128]{3,2,1,0:T(8,128)S(1)}, f32[2,256]{1,0:T(2,128)S(1)}) custom-call(s32[2,64,128]{2,1,0:T(8,128)} %labels_ref.1, f32[2,2,64,128]{3,2,1,0:T(8,128)} %jitter_ref.1, s32[64,128]{1,0:T(8,128)} %shells_ref.1, bf16[4,128,512]{2,1,0:T(8,128)(2,1)} %constant.4.clone.xtab_hbm, bf16[512,1024]{1,0:T(8,128)(2,1)} %constant.5.clone.ytab_hbm), custom_call_target="tpu_custom_call" | custom-call | tf_op jit(solution)/shard_map/exchange/pallas_call | solution.py:598
  46.0 1.5 %copy.9 = f32[38,2,64,128]{3,2,1,0:T(8,128)} copy(f32[38,2,64,128]{3,2,1,0:T(8,128)S(1)} %get-tuple-element.2) | data formatting | bytes 4980736
  47.4 0.6 %copy.10 = f32[2,256]{1,0:T(2,128)} copy(f32[2,256]{1,0:T(2,128)S(1)} %get-tuple-element.3) | data formatting | bytes 4096

commit v4 on v3

--- a/solution.py
+++ b/solution.py
@@ -207,10 +207,24 @@
         pl.semaphore_signal(
             barrier, 1, device_id={"row": shifted(row, step, rows)}, device_id_type=MESH
         )
-    for step in range(1, secs):
+    sec_steps = sorted({1, secs - 1})
+    remote = (sec >= 2) & (sec <= secs - 2)
+    for step in sec_steps:
         pl.semaphore_signal(
             barrier, 1, device_id={"sec": shifted(sec, step, secs)}, device_id_type=MESH
         )
+
+    @pl.when(hub)
+    def _():
+        for target in range(2, secs - 1):
+            pl.semaphore_signal(
+                barrier, 1, device_id={"sec": target}, device_id_type=MESH
+            )
+
+    @pl.when(remote)
+    def _():
+        pl.semaphore_signal(barrier, 1, device_id={"sec": 0}, device_id_type=MESH)
+
     for step in (1, -1):
         pl.semaphore_signal(
             barrier, 1, device_id={"col": shifted(col, step, cols)}, device_id_type=MESH
@@ -240,7 +254,9 @@
     )
     shell_own[...] = shells_ref[...].astype(jnp.float32).astype(jnp.bfloat16)
 
-    pl.semaphore_wait(barrier, rows + secs)
+    greeters = rows - 1 + len(sec_steps) + 2
+    extra = jnp.where(hub, max(secs - 3, 0), jnp.where(remote, 1, 0))
+    pl.semaphore_wait(barrier, greeters + extra)
 
     waits = []
 
@@ -290,6 +306,28 @@
             {"sec": shifted(sec, step, secs)},
         )
     plane_buf[row] = jnp.where(row < half, order_buf[0], order_buf[1])
+
+    xcopy.wait()
+    for step in order:
+        arrive(
+            plane_buf.at[shifted(row, -step, rows)],
+            p1_send.at[step - 1],
+            p1_recv.at[step - 1],
+            {"row": row},
+        )
+    half_step = jnp.dot(
+        xtab[...],
+        plane_buf[...].reshape(full_x, width_y),
+        preferred_element_type=jnp.float32,
+    )
+    half_send[...] = half_step.astype(jnp.bfloat16)
+    half_copy = transfer(
+        half_send, half_buf.at[sec], p2_send.at[0], p2_recv.at[from_sec], {"sec": 0}
+    )
+
+    @pl.when(sec > 0)
+    def _():
+        half_copy.start()
 
     for place in range(2):
         arrive(ybuf.at[place], y_send.at[place], y_recv.at[place], {"sec": sec})
@@ -345,28 +383,6 @@
         def _():
             for copy in next_copies:
                 copy.start()
-
-    xcopy.wait()
-    for step in order:
-        arrive(
-            plane_buf.at[shifted(row, -step, rows)],
-            p1_send.at[step - 1],
-            p1_recv.at[step - 1],
-            {"row": row},
-        )
-    half_step = jnp.dot(
-        xtab[...],
-        plane_buf[...].reshape(full_x, width_y),
-        preferred_element_type=jnp.float32,
-    )
-    half_send[...] = half_step.astype(jnp.bfloat16)
-    half_copy = transfer(
-        half_send, half_buf.at[sec], p2_send.at[0], p2_recv.at[from_sec], {"sec": 0}
-    )
-
-    @pl.when(sec > 0)
-    def _():
-        half_copy.start()
 
     for place in range(2):
         arrive(xbuf.at[place], x_send.at[place], x_recv.at[place], {"row": row})

time: 48.2 us -> 48.1 us (level)
  the two profiles are of different devices: /device:TPU:4 before, /device:TPU:2 now
where the time goes in v4:
time: 48.1 us; the launch traced here: 48 us
  Pallas kernels  45.3 us (94%)
  local copies, waits for them, and re-layouts  2.03 us (4%)
  between operations  0.64 us (1%)
    pallas_call x1, Pallas kernels, exchange(): pl.pallas_call(functools.partial(exchange_kernel, sizes), out_shape=(pltp...  45.3 us
    unnamed x2, local copies, waits for them, and re-layouts  2.03 us

profile of v4, /device:TPU:2, one launch (start us, length us, event | category | flops | bytes accessed | tf_op | source)
XLA Modules:
  0.0 48.0 jit_solution(14267143939113979120)
XLA Ops:
  0.6 45.3 %exchange.1 = (f32[38,2,64,128]{3,2,1,0:T(8,128)S(1)}, f32[2,256]{1,0:T(2,128)S(1)}) custom-call(s32[2,64,128]{2,1,0:T(8,128)} %labels_ref.1, f32[2,2,64,128]{3,2,1,0:T(8,128)} %jitter_ref.1, s32[64,128]{1,0:T(8,128)} %shells_ref.1, bf16[4,128,512]{2,1,0:T(8,128)(2,1)} %constant.4.clone.xtab_hbm, bf16[512,1024]{1,0:T(8,128)(2,1)} %constant.5.clone.ytab_hbm), custom_call_target="tpu_custom_call" | custom-call | tf_op jit(solution)/shard_map/exchange/pallas_call | solution.py:614
  46.0 1.5 %copy.9 = f32[38,2,64,128]{3,2,1,0:T(8,128)} copy(f32[38,2,64,128]{3,2,1,0:T(8,128)S(1)} %get-tuple-element.2) | data formatting | bytes 4980736
  47.4 0.6 %copy.10 = f32[2,256]{1,0:T(2,128)} copy(f32[2,256]{1,0:T(2,128)S(1)} %get-tuple-element.3) | data formatting | bytes 4096

commit v5 on v4

--- a/solution.py
+++ b/solution.py
@@ -329,6 +329,35 @@
     def _():
         half_copy.start()
 
+    mirror = rows - 1 - row
+    next_block = lax.rem(rows - row, half)
+    pair_copy = transfer(
+        shell_rows, shell_pair, s1_send.at[0], s1_recv.at[0], {"row": mirror}
+    )
+    next_copies = [
+        transfer(
+            shell_head,
+            shell_next,
+            s1_send.at[1 + place],
+            s1_recv.at[1],
+            {"row": target},
+        )
+        for place, target in enumerate((next_block, rows - 1 - next_block))
+    ]
+
+    @pl.when(hub)
+    def _():
+        shell_rows[0] = shell_own[...]
+        for source in range(1, secs):
+            arrive(shell_rows.at[source], s2_send.at[0], s2_recv.at[source - 1], {"sec": sec})
+        shell_head[...] = shell_rows[:, 0:16, :]
+        pair_copy.start()
+
+        @pl.when(row >= half)
+        def _():
+            for copy in next_copies:
+                copy.start()
+
     for place in range(2):
         arrive(ybuf.at[place], y_send.at[place], y_recv.at[place], {"sec": sec})
     lanes = flat.shape[0]
@@ -354,35 +383,6 @@
             x_recv.at[place],
             {"row": shifted(row, step, rows)},
         )
-
-    mirror = rows - 1 - row
-    next_block = lax.rem(rows - row, half)
-    pair_copy = transfer(
-        shell_rows, shell_pair, s1_send.at[0], s1_recv.at[0], {"row": mirror}
-    )
-    next_copies = [
-        transfer(
-            shell_head,
-            shell_next,
-            s1_send.at[1 + place],
-            s1_recv.at[1],
-            {"row": target},
-        )
-        for place, target in enumerate((next_block, rows - 1 - next_block))
-    ]
-
-    @pl.when(hub)
-    def _():
-        shell_rows[0] = shell_own[...]
-        for source in range(1, secs):
-            arrive(shell_rows.at[source], s2_send.at[0], s2_recv.at[source - 1], {"sec": sec})
-        shell_head[...] = shell_rows[:, 0:16, :]
-        pair_copy.start()
-
-        @pl.when(row >= half)
-        def _():
-            for copy in next_copies:
-                copy.start()
 
     for place in range(2):
         arrive(xbuf.at[place], x_send.at[place], x_recv.at[place], {"row": row})

time: 48.1 us -> 48.1 us (level)
  no operation moved by 1% of the time
where the time goes in v5:
time: 48.1 us; the launch traced here: 47.9 us
  Pallas kernels  45.2 us (94%)
  local copies, waits for them, and re-layouts  2.03 us (4%)
  between operations  0.64 us (1%)
    pallas_call x1, Pallas kernels, exchange(): pl.pallas_call(functools.partial(exchange_kernel, sizes), out_shape=(pltp...  45.2 us
    unnamed x2, local copies, waits for them, and re-layouts  2.03 us

profile of v5, /device:TPU:2, one launch (start us, length us, event | category | flops | bytes accessed | tf_op | source)
XLA Modules:
  0.0 47.9 jit_solution(1838502267259362674)
XLA Ops:
  0.6 45.2 %exchange.1 = (f32[38,2,64,128]{3,2,1,0:T(8,128)S(1)}, f32[2,256]{1,0:T(2,128)S(1)}) custom-call(s32[2,64,128]{2,1,0:T(8,128)} %labels_ref.1, f32[2,2,64,128]{3,2,1,0:T(8,128)} %jitter_ref.1, s32[64,128]{1,0:T(8,128)} %shells_ref.1, bf16[4,128,512]{2,1,0:T(8,128)(2,1)} %constant.4.clone.xtab_hbm, bf16[512,1024]{1,0:T(8,128)(2,1)} %constant.5.clone.ytab_hbm), custom_call_target="tpu_custom_call" | custom-call | tf_op jit(solution)/shard_map/exchange/pallas_call | solution.py:614
  45.9 1.5 %copy.9 = f32[38,2,64,128]{3,2,1,0:T(8,128)} copy(f32[38,2,64,128]{3,2,1,0:T(8,128)S(1)} %get-tuple-element.2) | data formatting | bytes 4980736
  47.3 0.6 %copy.10 = f32[2,256]{1,0:T(2,128)} copy(f32[2,256]{1,0:T(2,128)S(1)} %get-tuple-element.3) | data formatting | bytes 4096
